TPU v7x, 256 devices: a whole 4x4x8 slice. The times are simulated.
256 devices in a mesh: row: 32 (over z, y), col: 8 (over x, core).
Axes of the slice: x: 4, y: 4, z: 8, core: 2. Of those that a mesh axis runs over, the one named last changes fastest.
Arguments:
- inputs: bfloat16 [1024, 12288], P('row', 'col'), may hold values from -6 to 6
- hidden_pre: bfloat16 [1024, 24576], P(None, 'row'), may hold values from -8 to 8
- out_grad: bfloat16 [1024, 12288], P('row', 'col'), may hold values from -6 to 6
- weight_in: bfloat16 [12288, 24576], P('col', 'row'), may hold values from -0.0546875 to 0.0546875
- weight_out: bfloat16 [24576, 12288], P('row', 'col'), may hold values from -0.0390625 to 0.0390625
Outputs:
- grad_in: bfloat16 [1024, 12288], P('row', 'col')
- grad_weight_in: bfloat16 [12288, 24576], P('col', 'row')
- grad_weight_out: bfloat16 [24576, 12288], P('row', 'col')
All inputs are finite; a program needn't handle non-finite values.
Results may differ from a plain program's by a relative error of at most 0.0049.
Values may be sent and summed in bfloat16 or wider, within the bound.
A program may use at most 128 MiB of HBM per device.

v0:
```python
import jax
import jax.numpy as jnp
from jax import lax
from jax.sharding import PartitionSpec as P


def gelu_parts(hidden_pre):
    hval = hidden_pre.astype(jnp.float32)
    inner = 0.7978845608 * (hval + 0.044715 * hval * hval * hval)
    tval = jnp.tanh(inner)
    act = 0.5 * hval * (1.0 + tval)
    slope = 0.5 * (1.0 + tval) + 0.5 * hval * (1.0 - tval * tval) * 0.7978845608 * (
        1.0 + 3.0 * 0.044715 * hval * hval
    )
    return (act, slope)


def contract_rows(left, right):
    return lax.dot_general(
        left, right, (((0,), (0,)), ((), ())), preferred_element_type=jnp.float32
    )


def contract_cols(left, right):
    return lax.dot_general(
        left, right, (((1,), (1,)), ((), ())), preferred_element_type=jnp.float32
    )


def body(inputs, hidden_pre, out_grad, weight_in, weight_out):
    act, slope = gelu_parts(hidden_pre)
    act_b = act.astype(jnp.bfloat16)
    grad_all, input_all = (
        lax.all_gather(out_grad, "row", axis=0, tiled=True),
        lax.all_gather(inputs, "row", axis=0, tiled=True),
    )
    grad_weight_out = contract_rows(act_b, grad_all).astype(jnp.bfloat16)
    col_rows = grad_all.shape[0] // lax.axis_size("col")
    piece = grad_all
    d_act = lax.psum_scatter(
        contract_cols(piece, weight_out), "col", scatter_dimension=0, tiled=True
    )
    slope_mine = lax.dynamic_slice_in_dim(slope, lax.axis_index("col") * col_rows, col_rows, 0)
    d_mine = (d_act * slope_mine).astype(jnp.bfloat16)
    d_hid = lax.all_gather(d_mine, "col", axis=0, tiled=True)
    piece = d_hid
    grad_in = lax.psum_scatter(
        contract_cols(piece, weight_in), "row", scatter_dimension=0, tiled=True
    ).astype(jnp.bfloat16)
    grad_weight_in = contract_rows(input_all, d_hid).astype(jnp.bfloat16)
    return (grad_in, grad_weight_in, grad_weight_out)


def solution(mesh):
    return jax.shard_map(
        body,
        mesh=mesh,
        in_specs=(
            P("row", "col"),
            P(None, "row"),
            P("row", "col"),
            P("col", "row"),
            P("row", "col"),
        ),
        out_specs=(P("row", "col"), P("col", "row"), P("row", "col")),
        check_vma=False,
    )
```

profile of v0, /device:TPU:32, one launch (start us, length us, event | category | flops | bytes accessed | tf_op | source)
XLA Modules:
  0.0 479.8 jit_solution(16308524493274345741)
XLA Ops:
  7.2 0.0 copy-start
  7.2 0.0 all-gather.4.cloned.1.call-start
  7.2 0.7 all-gather.4.cloned.1.call-update
  7.9 0.0 reduce-scatter.3.cloned.1.call-start
  8.0 84.1 %all-gather.4.cloned.1.call-done = bf16[1024,1536]{1,0:T(8,128)(2,1)} async-done(((bf16[32,1536]{1,0:T(8,128)(2,1)}), bf16[1024,1536]{1,0:T(8,128)(2,1)}) %all-gather.4.cloned.1.call-update) | async-done | bytes 3145744 | tf_op jit(solution)/shard_map/all_gather | solution.py:34
  92.1 6.9 %fusion.12 = f32[1024,768]{1,0:T(8,128)} fusion(bf16[1024,1536]{1,0:T(8,128)(2,1)} %all-gather.4.cloned.1.call-done, bf16[768,1536]{1,0:T(8,128)(2,1)} %param.9), kind=kOutput, calls=%fused_computation.21 | convolution fusion | flops 2415919104 | bytes 8650752 | tf_op jit(solution)/shard_map/dot_general | solution.py:25
  99.0 0.0 reduce-scatter.3.cloned.1.call-update
  99.0 0.0 all-gather.6.cloned.1.call-start
  99.0 3.3 convert_element_type.21
  102.3 6.0 %fusion.1 = (f32[1024,768]{1,0:T(8,128)}, f32[1024,768]{1,0:T(8,128)}, f32[1024,768]{1,0:T(8,128)}) fusion(bf16[1024,768]{1,0:T(8,128)(2,1)} %param.6), kind=kLoop, calls=%fused_computation.4 | loop fusion | flops 6291456 | bytes 11010048 | tf_op jit(solution)/shard_map/tanh | solution.py:10
  108.3 26.5 %reduce-scatter.3.cloned.1.call-done = f32[128,768]{1,0:T(8,128)} async-done(((f32[1024,768]{1,0:T(8,128)}), f32[128,768]{1,0:T(8,128)}) %reduce-scatter.3.cloned.1.call-update) | async-done | bytes 393232 | tf_op jit(solution)/shard_map/reduce_scatter | solution.py:40
  134.8 2.3 fusion.7
  137.1 0.0 all-gather.6.cloned.1.call-update
  137.1 0.0 all-gather.8.cloned.1.call-start
  137.2 0.5 all-gather.8.cloned.1.call-update
  137.7 0.0 reduce-scatter.5.cloned.1.call-start
  137.8 25.2 %all-gather.6.cloned.1.call-done = bf16[1024,768]{1,0:T(8,128)(2,1)} async-done(((bf16[128,768]{1,0:T(8,128)(2,1)}), bf16[1024,768]{1,0:T(8,128)(2,1)}) %all-gather.6.cloned.1.call-update) | async-done | bytes 1572880 | tf_op jit(solution)/shard_map/all_gather | solution.py:45
  163.0 0.0 copy-done
  163.0 6.0 %fusion.13 = f32[1024,1536]{1,0:T(8,128)} fusion(bf16[1024,768]{1,0:T(8,128)(2,1)} %all-gather.6.cloned.1.call-done, bf16[1536,768]{1,0:T(8,128)(2,1)S(1)} %copy-done), kind=kOutput, calls=%fused_computation.22 | convolution fusion | flops 2415919104 | bytes 10223616 | tf_op jit(solution)/shard_map/dot_general | solution.py:25
  169.0 0.0 reduce-scatter.5.cloned.1.call-update
  169.0 6.7 %convolution_convert_fusion = bf16[768,1536]{1,0:T(8,128)(2,1)} fusion(bf16[1024,1536]{1,0:T(8,128)(2,1)} %all-gather.4.cloned.1.call-done, bf16[1024,768]{1,0:T(8,128)(2,1)} %param.6), kind=kOutput, calls=%fused_computation.1 | convolution fusion | flops 2424963072 | bytes 7077888 | tf_op jit(solution)/shard_map/dot_general | solution.py:19
  175.7 68.9 %all-gather.8.cloned.1.call-done = bf16[1024,1536]{1,0:T(8,128)(2,1)} async-done(((bf16[32,1536]{1,0:T(8,128)(2,1)}), bf16[1024,1536]{1,0:T(8,128)(2,1)}) %all-gather.8.cloned.1.call-update) | async-done | bytes 3145744 | tf_op jit(solution)/shard_map/all_gather | solution.py:35
  244.6 6.5 %fusion.2 = bf16[1536,768]{0,1:T(8,128)(2,1)} fusion(bf16[1024,768]{1,0:T(8,128)(2,1)} %all-gather.6.cloned.1.call-done, bf16[1024,1536]{1,0:T(8,128)(2,1)} %all-gather.8.cloned.1.call-done), kind=kOutput, calls=%fused_computation.6 | convolution fusion | flops 2417098752 | bytes 7077888 | tf_op jit(solution)/shard_map/dot_general | solution.py:19
  251.1 4.3 copy.8
  255.3 216.4 %reduce-scatter.5.cloned.1.call-done = f32[32,1536]{1,0:T(8,128)} async-done(((f32[1024,1536]{1,0:T(8,128)}), f32[32,1536]{1,0:T(8,128)}) %reduce-scatter.5.cloned.1.call-update) | async-done | bytes 196624 | tf_op jit(solution)/shard_map/reduce_scatter | solution.py:47
  471.7 1.6 convert_element_type.23
Async XLA Ops:
  7.2 155.8 %copy-start = (bf16[1536,768]{1,0:T(8,128)(2,1)S(1)}, bf16[1536,768]{1,0:T(8,128)(2,1)}, u32[]{:S(2)}) copy-start(bf16[1536,768]{1,0:T(8,128)(2,1)} %param.8) | copy-start | bytes 7077892
  7.2 84.9 %all-gather.4.cloned.1.call-start = ((), (), s32[]{:S(2)}) async-start(), calls=%async_computation.2 | async-start | bytes 3244032 | tf_op jit(solution)/shard_map/all_gather | solution.py:34
  7.9 126.9 %reduce-scatter.3.cloned.1.call-start = ((), (), s32[]{:S(2)}) async-start(), calls=%async_computation.3 | async-start | bytes 3538944 | tf_op jit(solution)/shard_map/reduce_scatter | solution.py:40
  99.0 64.0 %all-gather.6.cloned.1.call-start = ((), (), s32[]{:S(2)}) async-start(), calls=%async_computation.4 | async-start | bytes 1769472 | tf_op jit(solution)/shard_map/all_gather | solution.py:45
  137.1 107.4 %all-gather.8.cloned.1.call-start = ((), (), s32[]{:S(2)}) async-start(), calls=%async_computation.6 | async-start | bytes 3244032 | tf_op jit(solution)/shard_map/all_gather | solution.py:35
  137.7 334.0 %reduce-scatter.5.cloned.1.call-start = ((), (), s32[]{:S(2)}) async-start(), calls=%async_computation.5 | async-start | bytes 6488064 | tf_op jit(solution)/shard_map/reduce_scatter | solution.py:47
Sparse Core Ops, SparseCore 0:
  10.6 81.4 all-gather.3
  99.1 35.6 reduce-scatter.2
  137.3 25.6 all-gather.5
  165.4 79.1 all-gather.7
  248.4 223.2 reduce-scatter.4
where the time goes:
time: 481 us; the launch traced here: 480 us
  waiting for transfers between devices  422 us (88%)
  matrix products  26.1 us (5%)
  between operations  13.8 us (3%)
  other arithmetic  13.1 us (3%)
    reduce_scatter x1, waiting for transfers between devices, body(): lax.psum_scatter(contract_cols(piece, weight_in), 'row', scatter_dimensio...  216 us
    all_gather x1, waiting for transfers between devices, body(): lax.all_gather(out_grad, 'row', axis=0, tiled=True)  84.1 us
    all_gather x1, waiting for transfers between devices, body(): lax.all_gather(inputs, 'row', axis=0, tiled=True)  68.9 us
    reduce_scatter x1, waiting for transfers between devices, body(): lax.psum_scatter(contract_cols(piece, weight_out), 'col', scatter_dimensi...  26.5 us
    all_gather x1, waiting for transfers between devices, body(): d_hid = lax.all_gather(d_mine, 'col', axis=0, tiled=True)  25.2 us
    dot_general x2, matrix products, contract_rows(): lax.dot_general(left, right, (((0,), (0,)), ((), ())), preferred_element_...  13.2 us
    dot_general x2, matrix products, contract_cols(): lax.dot_general(left, right, (((1,), (1,)), ((), ())), preferred_element_...  12.9 us
  transfers between devices with their start and end apart: 5, of which 5 were waited for; matrix products, arithmetic and copies ran while one was open for 7% of the time, Pallas kernels for 0%

commit v1 on v0

v1 whole, which is shorter than its diff:
```python
import functools

import jax
import jax.numpy as jnp
from jax import lax
from jax.experimental import pallas as pl
from jax.experimental.pallas import tpu as pltpu
from jax.sharding import PartitionSpec as P

MESH = pl.DeviceIdType.MESH
F32, BF16 = jnp.float32, jnp.bfloat16
NT = (((1,), (1,)), ((), ()))
TN = (((0,), (0,)), ((), ()))
NN = (((1,), (0,)), ((), ()))


def gelu_terms(h):
    u = 0.7978845608 * (h + 0.044715 * h * h * h)
    return jnp.tanh(u)


def kernel(dims, inp, hid, grad, w_in, w_out, g_in, gw_in, gw_out,
           G, I, H, WI, WO, AT, D, PR, XS, XR, DH, PF, AS, AR, YB, YR, BS, BR, YA, AY, OUT, GI, GO,
           loc, out_sem, s_yo, r_yo, s_z, r_z, s_by, r_by, s_x, r_x):
    NZ, NY, NX, T, W, F = dims
    HOPS = NZ // 2
    QW = W // 4
    HW = W // 2
    row, col = lax.axis_index("row"), lax.axis_index("col")
    z, y = row // NY, row % NY
    x, c = col // 2, col % 2

    def zdev(sign):
        return (((z + sign + NZ) % NZ) * NY + y, col)

    def ydev(j):
        return (z * NY + (y + j) % NY, col)

    def xdev(j):
        return (row, ((x + j) % NX) * 2 + c)

    partner = (row, x * 2 + 1 - c)
    SIGN = (1, -1)

    def zoff(k):
        return (z + k + 2 * NZ) % NZ

    def yoff(k):
        return (y + k + 2 * NY) % NY

    def xoff(k):
        return (x + k + 2 * NX) % NX

    def limit(d, q):
        return HOPS if (q % 2 == 0) == (d == 0) else HOPS - 1

    def qs(q):
        return pl.ds(q * QW, QW)

    B = pl.ds(HW, HW)
    A = pl.ds(0, HW)

    def rcopy(src, dst, ssem, rsem, dev):
        return pltpu.make_async_remote_copy(src_ref=src, dst_ref=dst, send_sem=ssem, recv_sem=rsem,
                                            device_id=dev, device_id_type=MESH)

    sent = []

    def send(src, dst, ssem, rsem, dev):
        cp = rcopy(src, dst, ssem, rsem, dev)
        cp.start()
        sent.append(cp)

    def arrived(region, ssem, rsem, dev):
        rcopy(region, region, ssem, rsem, dev).wait_recv()

    def zi(p, d, q, h):
        return ((p * 2 + d) * 4 + q) * HOPS + h - 1

    loads = [
        pltpu.make_async_copy(grad, G.at[z, y], loc.at[0]),
        pltpu.make_async_copy(inp, I.at[z, y], loc.at[1]),
        pltpu.make_async_copy(hid, H, loc.at[2]),
        pltpu.make_async_copy(w_out, WO, loc.at[3]),
        pltpu.make_async_copy(w_in, WI, loc.at[4]),
    ]
    for cp in loads:
        cp.start()

    barrier = pltpu.get_barrier_semaphore()
    peers = [zdev(1), zdev(-1)] if NZ > 2 else [zdev(1)]
    peers += [ydev(j) for j in range(1, NY)] + [xdev(j) for j in range(1, NX)] + [partner]
    for dev in peers:
        pl.semaphore_signal(barrier, inc=1, device_id=dev, device_id_type=MESH)
    pl.semaphore_wait(barrier, len(peers))

    def gather(p, own, buf, load):
        NJ = NY - 1
        for j in range(1, NY):
            i = p * NJ + j - 1
            send(own, buf.at[z, y], s_yo.at[i], r_yo.at[i], ydev(j))
        for q in (2, 3):
            for d in (0, 1):
                if limit(d, q) >= 1:
                    i = zi(p, d, q, 1)
                    send(own.at[:, qs(q)], buf.at[z, y, :, qs(q)], s_z.at[i], r_z.at[i], zdev(SIGN[d]))
        yield
        load.wait()
        for j in range(1, NY):
            i = p * NJ + j - 1
            arrived(buf.at[z, yoff(-j)], s_yo.at[i], r_yo.at[i], ydev(j))
        for q in (0, 1):
            for d in (0, 1):
                if limit(d, q) >= 1:
                    i = zi(p, d, q, 1)
                    reg = buf.at[z, :, :, qs(q)]
                    send(reg, reg, s_z.at[i], r_z.at[i], zdev(SIGN[d]))
        yield
        for h in range(1, HOPS + 1):
            for pair in ((2, 3), (0, 1)):
                for q in pair:
                    for d in (0, 1):
                        if h > limit(d, q):
                            continue
                        zb = zoff(-SIGN[d] * h)
                        reg = buf.at[zb, y, :, qs(q)] if q >= 2 else buf.at[zb, :, :, qs(q)]
                        i = zi(p, d, q, h)
                        arrived(reg, s_z.at[i], r_z.at[i], zdev(SIGN[d]))
                        if h < limit(d, q):
                            i = zi(p, d, q, h + 1)
                            send(reg, reg, s_z.at[i], r_z.at[i], zdev(SIGN[d]))
                if pair == (2, 3):
                    for k in ((h, NZ - h) if h < HOPS else (h,)):
                        reg = buf.at[zoff(k), y, :, B]
                        for j in range(1, NY):
                            i = (p * NZ + k) * NJ + j - 1
                            send(reg, reg, s_by.at[i], r_by.at[i], ydev(j))
                yield
        for h in range(1, HOPS + 1):
            for k in ((h, NZ - h) if h < HOPS else (h,)):
                for j in range(1, NY):
                    i = (p * NZ + k) * NJ + j - 1
                    arrived(buf.at[zoff(k), yoff(-j), :, B], s_by.at[i], r_by.at[i], ydev(j))
            yield

    BT = NY * T

    def act_piece(i):
        h = H[pl.ds(pl.multiple_of(i * BT, BT), BT), :].astype(F32)
        t = gelu_terms(h)
        a = (0.5 * h * (1.0 + t)).astype(BF16)
        AT[:, pl.ds(pl.multiple_of(i * BT, BT), BT)] = a.T

    NTILE = 256

    def d_act_piece(i, xp):
        lhs = G[pl.ds(2 * xp, 2)].reshape(2 * BT, W)

        @pl.loop(0, F // NTILE)
        def _(n):
            cols = pl.ds(pl.multiple_of(n * NTILE, NTILE), NTILE)
            r = lax.dot_general(lhs, WO[cols, :], NT, preferred_element_type=F32)
            D[i, :, :, cols] = r.reshape(2, BT, NTILE)

    def gwo_piece(n):
        cols = pl.ds(pl.multiple_of(n * NTILE, NTILE), NTILE)
        rhs = G[:, :, :, cols].reshape(NZ * BT, NTILE)
        GO[:, cols] = lax.dot_general(AT[...], rhs, NN, preferred_element_type=F32).astype(BF16)

    def gwi_piece(n):
        cols = pl.ds(pl.multiple_of(n * NTILE, NTILE), NTILE)
        lhs = I[:, :, :, cols].reshape(NZ * BT, NTILE)
        GI[cols, :] = lax.dot_general(lhs, DH[...].reshape(NZ * BT, F), TN, preferred_element_type=F32).astype(BF16)

    def p_piece(blocks):
        vals = [DH[b] for b in blocks]
        lhs = vals[0] if len(vals) == 1 else jnp.concatenate(vals, axis=0)

        @pl.loop(0, W // NTILE)
        def _(n):
            cols = pl.ds(pl.multiple_of(n * NTILE, NTILE), NTILE)
            r = lax.dot_general(lhs, WI[cols, :], NT, preferred_element_type=F32)
            for m, b in enumerate(blocks):
                PF[b, :, :, cols] = r[m * BT:(m + 1) * BT].reshape(NY, T, NTILE)

    loads[2].wait()
    ag = gather(0, grad, G, loads[0])
    next(ag)
    done = 0
    for _ in ag:
        if done < NZ:
            act_piece(done)
            done += 1
    for i in range(done, NZ):
        act_piece(i)

    ag = gather(1, inp, I, loads[1])
    next(ag)
    step = lambda: next(ag, None)
    loads[3].wait()
    offs = {4: [2, 1, 3, 0], 2: [1, 0]}[NX]
    b_own = 2 * x + c

    def finish(i, off):
        k = i
        arrived(PR.at[i], s_x.at[k], r_x.at[k], partner)
        s = D[i, c] + PR[i]
        if off:
            XS[i] = s.astype(BF16)
            k = NX + i
            send(XS.at[i], XR.at[i], s_x.at[k], r_x.at[k], xdev(off))
            return
        for j in range(NX - 1):
            k = NX + j
            arrived(XR.at[j], s_x.at[k], r_x.at[k], xdev(offs[j]))
            s = s + XR[j].astype(F32)
        h = H[pl.ds(pl.multiple_of(b_own * BT, BT), BT), :].astype(F32)
        t = gelu_terms(h)
        slope = 0.5 * (1.0 + t) + 0.5 * h * (1.0 - t * t) * 0.7978845608 * (1.0 + 3.0 * 0.044715 * h * h)
        DH[b_own] = (s * slope).astype(BF16)
        reg = DH.at[b_own]
        for j in range(NX - 1):
            k = 2 * NX + j
            send(reg, reg, s_x.at[k], r_x.at[k], xdev(offs[j]))
        k = 3 * NX
        send(reg, reg, s_x.at[k], r_x.at[k], partner)

    for i, off in enumerate(offs):
        d_act_piece(i, xoff(off))
        send(D.at[i, 1 - c], PR.at[i], s_x.at[i], r_x.at[i], partner)
        step()
        if i > 0:
            finish(i - 1, offs[i - 1])
        step()
    n_go = W // NTILE
    go = 0
    while go < (n_go + 1) // 2:
        gwo_piece(go)
        go += 1
        step()
    finish(NX - 1, 0)
    step()
    while go < n_go:
        gwo_piece(go)
        go += 1
        step()
    go_out = pltpu.make_async_copy(GO, gw_out, out_sem.at[0])
    go_out.start()
    for j in (1, 0, 2) if NX == 4 else (0,):
        off = offs[j]
        k = 2 * NX + j
        reg = DH.at[2 * xoff(-off) + c]
        arrived(reg, s_x.at[k], r_x.at[k], xdev(off))
        k = 3 * NX + 1 + j
        send(reg, reg, s_x.at[k], r_x.at[k], partner)
        step()
    k = 3 * NX
    arrived(DH.at[2 * x + 1 - c], s_x.at[k], r_x.at[k], partner)
    for j in (1, 0, 2) if NX == 4 else (0,):
        k = 3 * NX + 1 + j
        arrived(DH.at[2 * xoff(-offs[j]) + 1 - c], s_x.at[k], r_x.at[k], partner)
    for _ in ag:
        pass

    loads[4].wait()
    NJ = NY - 1
    p = 2

    def rs_first(d):
        blocks = [zoff(d)] if d in (0, HOPS) else [zoff(d), zoff(-d)]
        p_piece(blocks)
        for k in ((d,) if d in (0, HOPS) else (d, NZ - d)):
            zb = zoff(k)
            YB[zb] = PF[zb, :, :, B].astype(BF16)
            for j in range(1, NY):
                i = (p * NZ + k) * NJ + j - 1
                send(YB.at[zb, yoff(j)], YR.at[k, j - 1], s_by.at[i], r_by.at[i], ydev(j))

    def rs_a(d):
        for q in (0, 1):
            for dr in (0, 1):
                if d > limit(dr, q):
                    continue
                v = PF[zoff(SIGN[dr] * d), :, :, qs(q)]
                if d + 1 <= limit(dr, q):
                    i = zi(p, dr, q, d + 1)
                    m = zi(0, dr, q, d + 1)
                    arrived(AR.at[m], s_z.at[i], r_z.at[i], zdev(SIGN[dr]))
                    v = v + AR[m].astype(F32)
                i = zi(p, dr, q, d)
                m = zi(0, dr, q, d)
                AS[m] = v.astype(BF16)
                send(AS.at[m], AR.at[m], s_z.at[i], r_z.at[i], zdev(SIGN[dr]))

    def y_sum(k):
        for j in range(1, NY):
            i = (p * NZ + k) * NJ + j - 1
            arrived(YR.at[k, j - 1], s_by.at[i], r_by.at[i], ydev(j))
        v = PF[zoff(k), y, :, B]
        for j in range(1, NY):
            v = v + YR[k, j - 1].astype(F32)
        return v

    def rs_b(d):
        for k in ((d,) if d in (0, HOPS) else (d, NZ - d)):
            v = y_sum(k)
            for q in (2, 3):
                vq = v[:, (q - 2) * QW:(q - 1) * QW]
                if d == 0:
                    for dr in (0, 1):
                        if limit(dr, q) >= 1:
                            i = zi(p, dr, q, 1)
                            m = zi(0, dr, q - 2, 1)
                            arrived(BR.at[m], s_z.at[i], r_z.at[i], zdev(SIGN[dr]))
                            vq = vq + BR[m].astype(F32)
                    OUT[:, qs(q)] = vq.astype(BF16)
                    continue
                for dr in (0, 1):
                    if d > limit(dr, q) or (k != d if dr == 0 else k != NZ - d):
                        continue
                    if d + 1 <= limit(dr, q):
                        i = zi(p, dr, q, d + 1)
                        m = zi(0, dr, q - 2, d + 1)
                        arrived(BR.at[m], s_z.at[i], r_z.at[i], zdev(SIGN[dr]))
                        vs = vq + BR[m].astype(F32)
                    else:
                        vs = vq
                    i = zi(p, dr, q, d)
                    m = zi(0, dr, q - 2, d)
                    BS[m] = vs.astype(BF16)
                    send(BS.at[m], BR.at[m], s_z.at[i], r_z.at[i], zdev(SIGN[dr]))

    gi = 0
    n_gi = W // NTILE
    for d in range(HOPS, -1, -1):
        rs_first(d)
        if d >= 1:
            rs_a(d)
        if d + 1 <= HOPS:
            rs_b(d + 1)
        if d < HOPS and gi < n_gi:
            gwi_piece(gi)
            gi += 1
    for q in (0, 1):
        v = PF[z, :, :, qs(q)]
        for dr in (0, 1):
            if limit(dr, q) >= 1:
                i = zi(p, dr, q, 1)
                m = zi(0, dr, q, 1)
                arrived(AR.at[m], s_z.at[i], r_z.at[i], zdev(SIGN[dr]))
                v = v + AR[m].astype(F32)
        PF[z, :, :, qs(q)] = v
        YA[:, :, qs(q)] = v.astype(BF16)
    for j in range(1, NY):
        i = p * NJ + j - 1
        send(YA.at[yoff(j)], AY.at[j - 1], s_yo.at[i], r_yo.at[i], ydev(j))
    while gi < n_gi:
        gwi_piece(gi)
        gi += 1
    gi_out = pltpu.make_async_copy(GI, gw_in, out_sem.at[1])
    gi_out.start()
    rs_b(0)
    v = PF[z, y, :, A]
    for j in range(1, NY):
        i = p * NJ + j - 1
        arrived(AY.at[j - 1], s_yo.at[i], r_yo.at[i], ydev(j))
        v = v + AY[j - 1].astype(F32)
    OUT[:, A] = v.astype(BF16)
    in_out = pltpu.make_async_copy(OUT, g_in, out_sem.at[2])
    in_out.start()
    for cp in sent:
        cp.wait_send()
    go_out.wait()
    gi_out.wait()
    in_out.wait()


def build(dims):
    NZ, NY, NX, T, W, F = dims
    HOPS, BT, NJ = NZ // 2, NY * T, NY - 1

    def body(inputs, hidden_pre, out_grad, weight_in, weight_out):
        any_spec = pl.BlockSpec(memory_space=pl.ANY)
        vm = pltpu.VMEM
        nz_sem = 3 * 2 * 4 * HOPS
        dma = pltpu.SemaphoreType.DMA
        return pl.pallas_call(
            functools.partial(kernel, dims),
            out_shape=(
                jax.ShapeDtypeStruct((T, W), BF16),
                jax.ShapeDtypeStruct((W, F), BF16),
                jax.ShapeDtypeStruct((F, W), BF16),
            ),
            in_specs=[any_spec] * 5,
            out_specs=(any_spec,) * 3,
            scratch_shapes=[
                vm((NZ, NY, T, W), BF16),
                vm((NZ, NY, T, W), BF16),
                vm((NZ * BT, F), BF16),
                vm((W, F), BF16),
                vm((F, W), BF16),
                vm((F, NZ * BT), BF16),
                vm((NX, 2, BT, F), F32),
                vm((NX, BT, F), F32),
                vm((NX - 1, BT, F), BF16),
                vm((NX - 1, BT, F), BF16),
                vm((NZ, BT, F), BF16),
                vm((NZ, NY, T, W), F32),
                vm((2 * 4 * HOPS, NY, T, W // 4), BF16),
                vm((2 * 4 * HOPS, NY, T, W // 4), BF16),
                vm((NZ, NY, T, W // 2), BF16),
                vm((NZ, NJ, T, W // 2), BF16),
                vm((2 * 4 * HOPS, T, W // 4), BF16),
                vm((2 * 4 * HOPS, T, W // 4), BF16),
                vm((NY, T, W // 2), BF16),
                vm((NJ, T, W // 2), BF16),
                vm((T, W), BF16),
                vm((W, F), BF16),
                vm((F, W), BF16),
                dma((5,)),
                dma((3,)),
                dma((3 * NJ,)), dma((3 * NJ,)),
                dma((nz_sem,)), dma((nz_sem,)),
                dma((3 * NZ * NJ,)), dma((3 * NZ * NJ,)),
                dma((4 * NX,)), dma((4 * NX,)),
            ],
            compiler_params=pltpu.CompilerParams(
                collective_id=0, has_side_effects=True, vmem_limit_bytes=60 * 2**20
            ),
        )(inputs, hidden_pre, out_grad, weight_in, weight_out)

    return body


def solution(mesh):
    return jax.shard_map(
        build((8, 4, 4, 32, 1536, 768)),
        mesh=mesh,
        in_specs=(
            P("row", "col"),
            P(None, "row"),
            P("row", "col"),
            P("col", "row"),
            P("row", "col"),
        ),
        out_specs=(P("row", "col"), P("col", "row"), P("row", "col")),
        check_vma=False,
    )
```

time: 481 us -> 117 us (0.24)
  waiting for transfers between devices: 422 us -> 0 us
  Pallas kernels: 0 us -> 108 us
  matrix products: 26.1 us -> 0 us
  between operations: 13.8 us -> 0.64 us
  other arithmetic: 13.1 us -> 0 us
    reduce_scatter x2 -> x0, waiting for transfers between devices: 243 us -> none  [the longest x1 216 us: body(): lax.psum_scatter(contract_cols(piece, weight_in), 'row', scatter_dimensio...]
    all_gather x3 -> x0, waiting for transfers between devices: 178 us -> none  [the longest x1 84.1 us: body(): lax.all_gather(out_grad, 'row', axis=0, tiled=True)]
    pallas_call x0 -> x1, Pallas kernels: none -> 108 us  [body(): pl.pallas_call(functools.partial(kernel, dims), out_shape=(jax.ShapeDtype...]
    dot_general x4 -> x0, matrix products: 26.1 us -> none  [the longest x2 13.2 us: contract_rows(): lax.dot_general(left, right, (((0,), (0,)), ((), ())), preferred_element_...]
    convert_element_type x3 -> x0, other arithmetic: 7.17 us -> none  [the longest x1 3.29 us: gelu_parts(): hval = hidden_pre.astype(jnp.float32)]
    tanh x1 -> x0, other arithmetic: 5.96 us -> none  [gelu_parts(): tval = jnp.tanh(inner)]
  transfers between devices with their start and end apart: 5 -> 0, of which waited for: 5 -> 0; matrix products, arithmetic and copies ran while one was open for 7% -> 0% of each run, Pallas kernels for 0% -> 0%
where the time goes in v1:
time: 117 us; the launch traced here: 115 us
  Pallas kernels  108 us (92%)
  local copies, waits for them, and re-layouts  6.32 us (5%)
    pallas_call x1, Pallas kernels, body(): pl.pallas_call(functools.partial(kernel, dims), out_shape=(jax.ShapeDtype...  108 us
    unnamed x5, local copies, waits for them, and re-layouts  6.32 us

profile of v1, /device:TPU:32, one launch (start us, length us, event | category | flops | bytes accessed | tf_op | source)
XLA Modules:
  0.0 115.1 jit_solution(8804001520172257698)
XLA Ops:
  0.6 108.1 %shard_map.76 = (bf16[32,1536]{1,0:T(8,128)(2,1)}, bf16[1536,768]{1,0:T(8,128)(2,1)}, bf16[768,1536]{1,0:T(8,128)(2,1)}) custom-call(bf16[32,1536]{1,0:T(8,128)(2,1)} %inp.1, bf16[1024,768]{1,0:T(8,128)(2,1)} %hid.1, bf16[32,1536]{1,0:T(8,128)(2,1)} %grad.1, bf16[1536,768]{1,0:T(8,128)(2,1)} %w_in.1, bf16[768,1536]{1,0:T(8,128)(2,1)} %w_out.1), custom_call_target="tpu_custom_call" | custom-call | tf_op jit(solution)/shard_map/pallas_call | solution.py:387
  108.8 1.5 %copy.11 = bf16[32,1536]{1,0:T(8,128)(2,1)} copy(bf16[32,1536]{1,0:T(8,128)(2,1)} %get-tuple-element.6) | data formatting | bytes 196608
  110.3 0.0 copy-start
  110.3 3.4 %copy.12 = bf16[1536,768]{1,0:T(8,128)(2,1)} copy(bf16[1536,768]{1,0:T(8,128)(2,1)} %get-tuple-element.7) | data formatting | bytes 4718592
  113.7 0.0 copy-done
  113.7 1.4 %copy.13 = bf16[768,1536]{1,0:T(8,128)(2,1)} copy(bf16[768,1536]{1,0:T(8,128)(2,1)S(1)} %copy-done) | data formatting | bytes 4718592
Async XLA Ops:
  110.3 3.4 %copy-start = (bf16[768,1536]{1,0:T(8,128)(2,1)S(1)}, bf16[768,1536]{1,0:T(8,128)(2,1)}, u32[]{:S(2)}) copy-start(bf16[768,1536]{1,0:T(8,128)(2,1)} %get-tuple-element.8) | copy-start | bytes 7077892

commit v2 on v0

v2 whole, which is shorter than its diff:
```python
import functools

import jax
import jax.numpy as jnp
from jax import lax
from jax.experimental import pallas as pl
from jax.experimental.pallas import tpu as pltpu
from jax.sharding import PartitionSpec as P

MESH = pl.DeviceIdType.MESH
F32, BF16 = jnp.float32, jnp.bfloat16
NT = (((1,), (1,)), ((), ()))
TN = (((0,), (0,)), ((), ()))
NN = (((1,), (0,)), ((), ()))
NTILE = 256
SIGN = (1, -1)

RATE = 45500.0
CORE_RATE = 650000.0
HOP, HOP2 = 2.4, 0.65
CORE_HOP = 1.0
PRIO1 = 0.6
GATE_Y, GATE_B, GATE_BY = ("arr", 0, 0, 0, 4, 2), ("By", 0, 3), ("By", 0, 4)


class Task:
    def __init__(self, name, deps=(), waits=(), sends=(), cost=0.05, prio=1, run=None):
        self.name, self.deps, self.waits, self.sends = name, tuple(deps), tuple(waits), tuple(sends)
        self.cost, self.prio, self.run = cost, prio, run


class Msg:
    def __init__(self, name, index, links, nbytes, make, region):
        self.name, self.index, self.links, self.nbytes = name, index, links, nbytes
        self.make, self.region = make, region


def order_of(tasks, msgs, loads):
    free = {}
    arrive = dict(loads)
    done, now, out = {}, 0.0, []
    left = list(tasks)
    while left:
        best, soonest = None, None
        for i, t in enumerate(left):
            if any(d not in done for d in t.deps) or any(w not in arrive for w in t.waits):
                continue
            ready = max([0.0] + [arrive[w] for w in t.waits])
            key = (t.prio, ready, i)
            if ready <= now and (best is None or key < best[0]):
                best = (key, i)
            if soonest is None or ready < soonest[0]:
                soonest = (ready, i)
        if best is None:
            now = max(now, soonest[0])
            continue
        t = left.pop(best[1])
        now += t.cost
        done[t.name] = now
        out.append(t)
        for m in t.sends:
            m = msgs[m]
            if m.links == ("core",):
                start = max(now, free.get("core", 0.0))
                free["core"] = start + m.nbytes / CORE_RATE
                arrive[m.name] = free["core"] + CORE_HOP
            else:
                end = 0.0
                for link in m.links:
                    free[link] = max(now, free.get(link, 0.0)) + m.nbytes / RATE
                    end = max(end, free[link])
                arrive[m.name] = end + HOP + (HOP2 if len(m.links) > 1 else 0.0)
    return out, now, done, arrive, free


def gelu_tanh(h):
    return jnp.tanh(0.7978845608 * (h + 0.044715 * h * h * h))


def plan(dims, pos, r):
    NZ, NY, NX, T, W, F, bounds, NA = dims
    NQ = len(bounds) - 1
    z, y, x, c = pos
    HOPS, BT, XT, FH, WH = NZ // 2, NY * T, NY * T // NX, F // 2, W // 2
    tasks, msgs = [], {}

    def task(name, **kw):
        tasks.append(Task(name, **kw))
        return name

    def msg(name, links, nbytes, make, region):
        msgs[name] = Msg(name, len(msgs), links, nbytes, make, region)
        return name

    def qs(q):
        return pl.ds(bounds[q], bounds[q + 1] - bounds[q])

    def qw(q):
        return bounds[q + 1] - bounds[q]

    def mod(v, n):
        return (v + 4 * n) % n

    def zdev(s):
        return {"row": mod(z + s, NZ) * NY + y}

    def ydev(s):
        return {"row": z * NY + mod(y + s, NY)}

    def xdev(s):
        return {"col": mod(x + s, NX) * 2 + c}

    core = {"col": x * 2 + 1 - c}
    zof, yof, xof = (lambda k: mod(z + k, NZ)), (lambda k: mod(y + k, NY)), (lambda k: mod(x + k, NX))
    ZL, YL = ("z+", "z-"), ("y+", "y-")

    def xlinks(j):
        return ("x+",) if j == 1 else ("x-",) if j == NX - 1 else ("x+", "x-")

    A, B = pl.ds(0, bounds[NA]), pl.ds(bounds[NA], W - bounds[NA])
    AW, BW = bounds[NA], W - bounds[NA]
    mid = bounds[NA // 2]
    GA = (pl.ds(0, mid), pl.ds(mid, AW - mid))
    GB = (qs(NA), qs(NA + 1))
    QA, QB = tuple(range(NA)), (NA, NA + 1)
    YD = ((1, 0), (3, 1), (2, None))

    def half(v):
        return pl.ds(pl.multiple_of(v * FH, 128), FH)

    def limit(d, q):
        return HOPS if (q % 2 == 0) == (d == 0) else HOPS - 1

    def chains(q):
        return [(d, h) for d in (0, 1) for h in range(1, limit(d, q) + 1)]

    def gather(p, own, buf, gate_y, gate_b, gate_by):
        ld = ("load", p)
        for j, d in YD:
            msg(("yo", p, j), YL if d is None else (YL[d],), T * AW * 2,
                lambda j=j: (r[own].at[:, A], r[buf].at[z, y, :, A], ydev(j)), lambda j=j: r[buf].at[z, yof(-j), :, A])
        yo = [("yo", p, j) for j in (1, 3, 2)]
        task(("y", p), deps=gate_y, sends=yo, prio=0)
        for i in range(4):
            for q in (0, 1):
                cols = pl.ds(q * WH, WH) if i == 0 else GA[q]
                pick = lambda b, i=i, cols=cols: r[buf].at[b, yof(-i), :, cols]
                for d, h in chains(q):
                    s = SIGN[d]
                    zb = lambda k, s=s: zof(-s * k)
                    if i == 0 and h == 1:
                        make = lambda s=s, pick=pick, cols=cols: (r[own].at[:, cols], pick(z), zdev(s))
                    else:
                        make = lambda h=h, s=s, pick=pick, zb=zb: (pick(zb(h - 1)), pick(zb(h - 1)), zdev(s))
                    msg(("gz", p, d, q, h, i), (ZL[d],), T * cols.size * 2, make, lambda h=h, pick=pick, zb=zb: pick(zb(h)))
                    nxt = [("gz", p, d, q, h + 1, i)] if h < limit(d, q) else []
                    dep = ("arr", p, d, q, h - 1, i) if h > 1 else ("zA", p, i) if i else ("zB", p)
                    task(("arr", p, d, q, h, i), waits=[("gz", p, d, q, h, i)], sends=nxt, prio=0 + p * PRIO1, deps=[dep])
        first = lambda i: [("gz", p, d, q, 1, i) for q in (0, 1) for d in (0, 1) if limit(d, q) >= 1]
        task(("zB", p), deps=gate_b, sends=first(0), prio=0)
        for i in (1, 3, 2):
            task(("zA", p, i), deps=[("y", p)], waits=[("yo", p, i)], sends=first(i), prio=0)
        for k in range(NZ):
            come = [[], []]
            for i in range(4 if k else 0):
                for q in (0, 1):
                    at = ("arr", p, 1, q, k, i) if k <= limit(1, q) else ("arr", p, 0, q, NZ - k, i)
                    come[i > 0].append(at)
            for d in (0, 1):
                s = SIGN[d]
                msg(("by", p, k, d), (YL[d],), T * BW * 2,
                    lambda s=s, k=k: (r[buf].at[zof(k), y, :, B] if k else r[own].at[:, B], r[buf].at[zof(k), y, :, B], ydev(s)),
                    lambda s=s, k=k: r[buf].at[zof(k), yof(-s), :, B])
                fwd = lambda s, k, cols: r[buf].at[zof(k), yof(-s), :, cols]
                cols = GB[d]
                msg(("byr", p, k, d), (YL[d],), T * cols.size * 2,
                    lambda s=s, k=k, cols=cols, fwd=fwd: (fwd(s, k, cols), fwd(s, k, cols), ydev(s)),
                    lambda k=k, cols=cols: r[buf].at[zof(k), yof(-2), :, cols])
            task(("By", p, k), deps=(come[0] if k else [("y", p)]) + gate_by,
                 sends=[("by", p, k, 0), ("by", p, k, 1)], prio=p * PRIO1)
            for d in (0, 1):
                task(("Byr", p, k, d), deps=[("By", p, k)], waits=[("by", p, k, d)], sends=[("byr", p, k, d)],
                     prio=p * PRIO1)
            task(("blk", p, k), deps=(come[1] if k else [("zA", p, i) for i in (1, 2, 3)]) + [("Byr", p, k, 0), ("Byr", p, k, 1)],
                 waits=[("byr", p, k, 0), ("byr", p, k, 1)] + ([] if k else [ld]), prio=p * PRIO1)

    gather(0, "grad", "G", [], [], [])
    known = {t.name for t in tasks}
    gates = [[g] if g in known else [("zB", 0)] for g in (GATE_Y, GATE_B, GATE_BY)]
    gather(1, "inp", "I", *gates)
    for i in range(2, 5):
        task(("ld", i), waits=[("load", i)], cost=0, prio=1)

    def dot_d(k):
        zb = zof(k)
        lhs = r["G"][zb].reshape(BT, W)

        @pl.loop(0, F // NTILE)
        def _(n):
            cols = pl.ds(pl.multiple_of(n * NTILE, NTILE), NTILE)
            v = lax.dot_general(lhs, r["WO"][cols, :], NT, preferred_element_type=F32)
            r["D"][zb, :, :, cols] = v.reshape(NX, XT, NTILE)

    def sum_core(k):
        r["XS"][k] = r["D"][zof(k), :, :, half(c)] + r["PR"][k]

    def make_dh(k):
        v = r["XS"][k, x]
        for j in range(1, NX):
            v = v + r["XR"][k, j - 1]
        zb = zof(k)
        h = r["H"][pl.ds(pl.multiple_of(zb * BT + x * XT, XT), XT), half(c)].astype(F32)
        t = gelu_tanh(h)
        slope = 0.5 * (1.0 + t) + 0.5 * h * (1.0 - t * t) * 0.7978845608 * (1.0 + 3.0 * 0.044715 * h * h)
        r["DH"][zb, x, :, half(c)] = (v * slope).astype(BF16)

    for k in range(NZ):
        msg(("pair", k), ("core",), BT * FH * 4,
            lambda k=k: (r["D"].at[zof(k), :, :, half(1 - c)], r["PR"].at[k], core), lambda k=k: r["PR"].at[k])
        for j in range(1, NX):
            msg(("xs", k, j), xlinks(j), XT * FH * 4,
                lambda k=k, j=j: (r["XS"].at[k, xof(j)], r["XR"].at[k, j - 1], xdev(j)), lambda k=k, j=j: r["XR"].at[k, j - 1])
            msg(("dh", k, j), xlinks(j), XT * FH * 2,
                lambda k=k, j=j: (r["DH"].at[zof(k), x, :, half(c)], r["DH"].at[zof(k), x, :, half(c)], xdev(j)),
                lambda k=k, j=j: r["DH"].at[zof(k), xof(-j), :, half(c)])
        msg(("df", k), ("core",), BT * FH * 2,
            lambda k=k: (r["DH"].at[zof(k), :, :, half(c)], r["DH"].at[zof(k), :, :, half(c)], core),
            lambda k=k: r["DH"].at[zof(k), :, :, half(1 - c)])
        peers = range(1, NX)
        task(("d", k), deps=[("blk", 0, k), ("ld", 3)], sends=[("pair", k)], cost=1.2, prio=1, run=lambda k=k: dot_d(k))
        task(("s", k), deps=[("d", k)], waits=[("pair", k)], sends=[("xs", k, j) for j in peers], cost=0.3, prio=0.5,
             run=lambda k=k: sum_core(k))
        task(("h", k), deps=[("s", k), ("ld", 2)], waits=[("xs", k, j) for j in peers],
             sends=[("dh", k, j) for j in peers], cost=0.3, prio=0.5, run=lambda k=k: make_dh(k))
        task(("f", k), deps=[("h", k)], waits=[("dh", k, j) for j in peers], sends=[("df", k)], prio=0.5)
        task(("e", k), deps=[("f", k)], waits=[("df", k)], prio=0.5)

    def dot_p(k):
        zb = zof(k)
        lhs = r["DH"][zb].reshape(BT, F)

        @pl.loop(0, W // NTILE)
        def _(n):
            cols = pl.ds(pl.multiple_of(n * NTILE, NTILE), NTILE)
            v = lax.dot_general(lhs, r["WI"][cols, :], NT, preferred_element_type=F32)
            r["PF"][zb, :, :, cols] = v.reshape(NY, T, NTILE)

    def ystage(key, k, qq, dep, cost):
        slot = k
        off = bounds[qq[0]]
        loc = lambda q: pl.ds(bounds[q] - off, qw(q))

        def put(i, who, q, extra=None):
            v = r["PF"][zof(k), yof(who), :, qs(q)]
            if extra is not None:
                v = v + r["YR"][slot, extra, :, loc(q)].astype(F32)
            r["YS"][slot, i, :, loc(q)] = v.astype(BF16)

        for d in (0, 1):
            s, mine, other = SIGN[d], qq[d], qq[1 - d]
            for kind, q, i in (("r", mine, 0), ("n", mine, 1 + d), ("m", other, 1 + d)):
                mk = lambda i=i, q=q, s=s: (r["YS"].at[slot, i, :, loc(q)], r["YR"].at[slot, i, :, loc(q)], ydev(s))
                msg((kind, key, d), (YL[d],), T * qw(q) * 2, mk, lambda i=i, q=q: r["YR"].at[slot, i, :, loc(q)])

        def start():
            for d in (0, 1):
                put(0, 2, qq[d])
                put(1 + d, SIGN[d], qq[1 - d])

        task(("ys", key), deps=dep, sends=[("r", key, 0), ("r", key, 1), ("m", key, 0), ("m", key, 1)], cost=cost,
             prio=0.5, run=start)
        for d in (0, 1):
            task(("yc", key, d), deps=[("ys", key)], waits=[("r", key, d)], sends=[("n", key, d)], prio=0.3,
                 run=lambda d=d: put(1 + d, SIGN[d], qq[d], 0))

        def total():
            w = qw(qq[0]) + qw(qq[1])
            v = r["PF"][zof(k), y, :, pl.ds(off, w)]
            for i in (1, 2):
                v = v + r["YR"][slot, i, :, pl.ds(0, w)].astype(F32)
            return v

        return [(kind, key, d) for kind in ("n", "m") for d in (0, 1)], total

    order = [HOPS]
    for d in range(HOPS - 1, 0, -1):
        order += [d, NZ - d]
    order.append(0)
    tag = lambda q, d, h: (d * NA + q % NA) * HOPS + h - 1

    for q in range(NQ):
        for d, h in chains(q):
            s = SIGN[d]
            bs, br = ("AS", "AR") if q < NA else ("BS", "BR")
            cut = (lambda ref, m, q=q: ref.at[m, :, :, pl.ds(0, qw(q))]) if q < NA else (
                lambda ref, m, q=q: ref.at[m, :, pl.ds(0, qw(q))])
            m = tag(q, d, h)
            msg(("rz", d, q, h), (ZL[d],), (BT if q < NA else T) * qw(q) * 2,
                lambda m=m, s=s, bs=bs, br=br, cut=cut: (cut(r[bs], m), cut(r[br], m), zdev(s)),
                lambda m=m, br=br, cut=cut: cut(r[br], m))

    def step_a(d, q, h):
        v = r["PF"][zof(SIGN[d] * h), :, :, qs(q)]
        if h < limit(d, q):
            v = v + r["AR"][tag(q, d, h + 1), :, :, pl.ds(0, qw(q))].astype(F32)
        r["AS"][tag(q, d, h), :, :, pl.ds(0, qw(q))] = v.astype(BF16)

    def step_b(d, q, h, k):
        v = r["VB"][k, :, pl.ds(bounds[q] - bounds[NA], qw(q))]
        if h < limit(d, q):
            v = v + r["BR"][tag(q, d, h + 1), :, pl.ds(0, qw(q))].astype(F32)
        r["BS"][tag(q, d, h), :, pl.ds(0, qw(q))] = v.astype(BF16)

    for n, k in enumerate(order):
        task(("p", k), deps=[("e", k), ("ld", 4)], cost=1.2, prio=1 + 0.01 * n, run=lambda k=k: dot_p(k))
        waits, total = ystage(k, k, QB, [("p", k)], 0.2)

        def hold(k=k, total=total):
            r["VB"][k] = total()

        task(("v", k), deps=[("yc", k, 0), ("yc", k, 1)], waits=waits, cost=0.1, prio=0.4, run=hold)
        for q in range(NQ):
            for d, h in chains(q):
                if (h if d == 0 else NZ - h) != k:
                    continue
                waits = [("rz", d, q, h + 1)] if h < limit(d, q) else []
                dep = [("rzt", d, q, h + 1)] if h < limit(d, q) else []
                if q < NA:
                    task(("rzt", d, q, h), deps=dep + [("p", k)], waits=waits, sends=[("rz", d, q, h)], cost=0.12,
                         prio=0.3, run=lambda d=d, q=q, h=h: step_a(d, q, h))
                else:
                    task(("rzt", d, q, h), deps=dep + [("v", k)], waits=waits, sends=[("rz", d, q, h)], cost=0.05,
                         prio=0.3, run=lambda d=d, q=q, h=h, k=k: step_b(d, q, h, k))

    def last_a():
        for q in QA:
            v = r["PF"][z, :, :, qs(q)]
            for d in (0, 1):
                if limit(d, q) >= 1:
                    v = v + r["AR"][tag(q, d, 1), :, :, pl.ds(0, qw(q))].astype(F32)
            r["PF"][z, :, :, qs(q)] = v
            r["YA"][:, :, qs(q)] = v.astype(BF16)

    lasts = lambda qq: [("rz", d, q, 1) for q in qq for d in (0, 1) if limit(d, q) >= 1]
    sent = lambda qq: [("rzt",) + m[1:] for m in lasts(qq)]
    task("sumA", deps=[("p", 0)] + sent(QA), waits=lasts(QA), sends=[("ya", j) for j in (1, 3, 2)], cost=0.3, prio=0.3, run=last_a)
    for j, d in YD:
        msg(("ya", j), YL if d is None else (YL[d],), T * AW * 2,
            lambda j=j: (r["YA"].at[yof(j)], r["AY"].at[j - 1], ydev(j)), lambda j=j: r["AY"].at[j - 1])

    def out_a():
        v = r["PF"][z, y, :, A]
        for j in (1, 2, 3):
            v = v + r["AY"][j - 1].astype(F32)
        r["OUT"][:, A] = v.astype(BF16)

    task("outA", deps=["sumA"], waits=[("ya", j) for j in (1, 3, 2)], cost=0.1, prio=0.3, run=out_a)

    def out_b():
        for q in QB:
            v = r["VB"][0, :, pl.ds(bounds[q] - bounds[NA], qw(q))]
            for d in (0, 1):
                if limit(d, q) >= 1:
                    v = v + r["BR"][tag(q, d, 1), :, pl.ds(0, qw(q))].astype(F32)
            r["OUT"][:, qs(q)] = v.astype(BF16)

    task("outB", deps=[("v", 0)] + sent(QB), waits=lasts(QB), cost=0.1, prio=0.3, run=out_b)
    task("out", deps=["outA", "outB"], cost=0.05, run=lambda: r["store"](2))

    def act_piece(i):
        rows = pl.ds(i * BT, BT)
        h = r["H"][rows, :].astype(F32)
        r["AT"][:, rows] = (0.5 * h * (1.0 + gelu_tanh(h))).astype(BF16).T

    def gwo_piece(n):
        cols = pl.ds(n * NTILE, NTILE)
        rhs = r["G"][:, :, :, cols].reshape(NZ * BT, NTILE)
        r["GO"][:, cols] = lax.dot_general(r["AT"][...], rhs, NN, preferred_element_type=F32).astype(BF16)

    def gwi_piece(n):
        cols = pl.ds(n * NTILE, NTILE)
        lhs = r["I"][:, :, :, cols].reshape(NZ * BT, NTILE)
        rhs = r["DH"][...].reshape(NZ * BT, F)
        r["GI"][cols, :] = lax.dot_general(lhs, rhs, TN, preferred_element_type=F32).astype(BF16)

    for i in range(NZ):
        task(("act", i), deps=[("ld", 2)], cost=0.6, prio=5, run=lambda i=i: act_piece(i))
    for n in range(W // NTILE):
        task(("go", n), deps=[("blk", 0, k) for k in range(NZ)] + [("act", i) for i in range(NZ)], cost=0.9, prio=6,
             run=lambda n=n: gwo_piece(n))
    task("goout", deps=[("go", n) for n in range(W // NTILE)], prio=6, run=lambda: r["store"](0))
    for n in range(W // NTILE):
        task(("gi", n), deps=[("blk", 1, k) for k in range(NZ)] + [("e", k) for k in range(NZ)], cost=1.0, prio=7,
             run=lambda n=n: gwi_piece(n))
    task("giout", deps=[("gi", n) for n in range(W // NTILE)], prio=7, run=lambda: r["store"](1))
    return tasks, msgs


@functools.lru_cache(None)
def n_msgs(dims):
    return len(plan(dims, (0, 0, 0, 0), {})[1])


LOADS = {("load", 0): 0.5, ("load", 1): 0.5, ("load", 2): 1.5, ("load", 3): 3.0, ("load", 4): 4.5}
NAMES = ("inp", "hid", "grad", "w_in", "w_out", "g_in", "gw_in", "gw_out", "G", "I", "H", "WI", "WO", "AT", "D", "PR", "XS",
         "XR", "DH", "PF", "AS", "AR", "YS", "YR", "YA", "AY", "VB", "BS", "BR", "OUT", "GI", "GO", "loc", "osem", "ss", "rs")


def kernel(dims, *refs):
    NZ, NY, NX = dims[:3]
    r = dict(zip(NAMES, refs, strict=True))
    row, col = lax.axis_index("row"), lax.axis_index("col")
    z, y, x, c = row // NY, row % NY, col // 2, col % 2

    copies = [(r["grad"], r["G"].at[z, y]), (r["inp"], r["I"].at[z, y]), (r["hid"], r["H"]), (r["w_out"], r["WO"]),
              (r["w_in"], r["WI"])]
    copies = [pltpu.make_async_copy(a, b, r["loc"].at[i]) for i, (a, b) in enumerate(copies)]
    for cp in copies:
        cp.start()
    stores = [pltpu.make_async_copy(a, b, r["osem"].at[i]) for i, (a, b) in enumerate(
        [(r["GO"], r["gw_out"]), (r["GI"], r["gw_in"]), (r["OUT"], r["g_in"])])]
    r["store"] = lambda i: stores[i].start()

    tasks, msgs = plan(dims, (z, y, x, c), r)
    order = order_of(tasks, msgs, LOADS)[0]

    barrier = pltpu.get_barrier_semaphore()
    rows = [((z + s + NZ) % NZ) * NY + y for s in (1, -1)] + [z * NY + (y + s + NY) % NY for s in (1, -1)]
    cols = [((x + j) % NX) * 2 + c for j in range(1, NX)] + [x * 2 + 1 - c]
    rows.append(z * NY + (y + 2) % NY)
    peers = [{"row": v} for v in rows] + [{"col": v} for v in cols]
    for dev in peers:
        pl.semaphore_signal(barrier, inc=1, device_id=dev, device_id_type=MESH)
    pl.semaphore_wait(barrier, len(peers))

    def rcopy(m, src, dst, dev):
        return pltpu.make_async_remote_copy(src_ref=src, dst_ref=dst, send_sem=r["ss"].at[m.index],
                                            recv_sem=r["rs"].at[m.index], device_id=dev, device_id_type=MESH)

    started = []
    for t in order:
        for w in t.waits:
            if w[0] == "load":
                copies[w[1]].wait()
            else:
                m = msgs[w]
                region = m.region()
                rcopy(m, region, region, m.make()[2]).wait_recv()
        if t.run is not None:
            t.run()
        for s in t.sends:
            cp = rcopy(msgs[s], *msgs[s].make())
            cp.start()
            started.append(cp)
    for cp in started:
        cp.wait_send()
    for cp in stores:
        cp.wait()


def build(dims):
    NZ, NY, NX, T, W, F, bounds, NA = dims
    HOPS, BT = NZ // 2, NY * T
    XT, FH = BT // NX, F // 2
    AW, BW = bounds[NA], W - bounds[NA]
    QA = max(bounds[i + 1] - bounds[i] for i in range(NA))
    QB = max(bounds[NA + 1] - bounds[NA], W - bounds[NA + 1])

    def body(inputs, hidden_pre, out_grad, weight_in, weight_out):
        any_spec = pl.BlockSpec(memory_space=pl.ANY)
        vm, dma, n = pltpu.VMEM, pltpu.SemaphoreType.DMA, n_msgs(dims)
        return pl.pallas_call(
            functools.partial(kernel, dims),
            out_shape=(
                jax.ShapeDtypeStruct((T, W), BF16),
                jax.ShapeDtypeStruct((W, F), BF16),
                jax.ShapeDtypeStruct((F, W), BF16),
            ),
            in_specs=[any_spec] * 5,
            out_specs=(any_spec,) * 3,
            scratch_shapes=[
                vm((NZ, NY, T, W), BF16),
                vm((NZ, NY, T, W), BF16),
                vm((NZ * BT, F), BF16),
                vm((W, F), BF16),
                vm((F, W), BF16),
                vm((F, NZ * BT), BF16),
                vm((NZ, NX, XT, F), F32),
                vm((NZ, NX, XT, FH), F32),
                vm((NZ, NX, XT, FH), F32),
                vm((NZ, NX - 1, XT, FH), F32),
                vm((NZ, NX, XT, F), BF16),
                vm((NZ, NY, T, W), F32),
                vm((2 * NA * HOPS, NY, T, QA), BF16),
                vm((2 * NA * HOPS, NY, T, QA), BF16),
                vm((NZ, 3, T, BW), BF16),
                vm((NZ, 3, T, BW), BF16),
                vm((NY, T, AW), BF16),
                vm((NY - 1, T, AW), BF16),
                vm((NZ, T, BW), F32),
                vm((2 * NA * HOPS, T, QB), BF16),
                vm((2 * NA * HOPS, T, QB), BF16),
                vm((T, W), BF16),
                vm((W, F), BF16),
                vm((F, W), BF16),
                dma((5,)),
                dma((3,)),
                dma((n,)),
                dma((n,)),
            ],
            compiler_params=pltpu.CompilerParams(
                collective_id=0, has_side_effects=True, vmem_limit_bytes=60 * 2**20
            ),
        )(inputs, hidden_pre, out_grad, weight_in, weight_out)

    return body


def solution(mesh):
    return jax.shard_map(
        build((8, 4, 4, 32, 1536, 768, (0, 256, 384, 512, 640, 1024, 1536), 4)),
        mesh=mesh,
        in_specs=(
            P("row", "col"),
            P(None, "row"),
            P("row", "col"),
            P("col", "row"),
            P("row", "col"),
        ),
        out_specs=(P("row", "col"), P("col", "row"), P("row", "col")),
        check_vma=False,
    )
```

time: 481 us -> 95 us (0.20)
  waiting for transfers between devices: 422 us -> 0 us
  Pallas kernels: 0 us -> 87.4 us
  matrix products: 26.1 us -> 0 us
  between operations: 13.8 us -> 0.64 us
  other arithmetic: 13.1 us -> 0 us
    reduce_scatter x2 -> x0, waiting for transfers between devices: 243 us -> none  [the longest x1 216 us: body(): lax.psum_scatter(contract_cols(piece, weight_in), 'row', scatter_dimensio...]
    all_gather x3 -> x0, waiting for transfers between devices: 178 us -> none  [the longest x1 84.1 us: body(): lax.all_gather(out_grad, 'row', axis=0, tiled=True)]
    pallas_call x0 -> x1, Pallas kernels: none -> 87.4 us  [body(): pl.pallas_call(functools.partial(kernel, dims), out_shape=(jax.ShapeDtype...]
    dot_general x4 -> x0, matrix products: 26.1 us -> none  [the longest x2 13.2 us: contract_rows(): lax.dot_general(left, right, (((0,), (0,)), ((), ())), preferred_element_...]
    convert_element_type x3 -> x0, other arithmetic: 7.17 us -> none  [the longest x1 3.29 us: gelu_parts(): hval = hidden_pre.astype(jnp.float32)]
    tanh x1 -> x0, other arithmetic: 5.96 us -> none  [gelu_parts(): tval = jnp.tanh(inner)]
  transfers between devices with their start and end apart: 5 -> 0, of which waited for: 5 -> 0; matrix products, arithmetic and copies ran while one was open for 7% -> 0% of each run, Pallas kernels for 0% -> 0%
where the time goes in v2:
time: 95 us; the launch traced here: 94.3 us
  Pallas kernels  87.4 us (92%)
  local copies, waits for them, and re-layouts  6.32 us (7%)
    pallas_call x1, Pallas kernels, body(): pl.pallas_call(functools.partial(kernel, dims), out_shape=(jax.ShapeDtype...  87.4 us
    unnamed x5, local copies, waits for them, and re-layouts  6.32 us

profile of v2, /device:TPU:32, one launch (start us, length us, event | category | flops | bytes accessed | tf_op | source)
XLA Modules:
  0.0 94.3 jit_solution(12327598901059226301)
XLA Ops:
  0.6 87.4 %shard_map.76 = (bf16[32,1536]{1,0:T(8,128)(2,1)}, bf16[1536,768]{1,0:T(8,128)(2,1)}, bf16[768,1536]{1,0:T(8,128)(2,1)}) custom-call(bf16[32,1536]{1,0:T(8,128)(2,1)} %refs_0_.1, bf16[1024,768]{1,0:T(8,128)(2,1)} %refs_1_.1, bf16[32,1536]{1,0:T(8,128)(2,1)} %refs_2_.1, bf16[1536,768]{1,0:T(8,128)(2,1)} %refs_3_.1, bf16[768,1536]{1,0:T(8,128)(2,1)} %refs_4_.1), custom_call_target="tpu_custom_call" | custom-call | tf_op jit(solution)/shard_map/pallas_call | solution.py:472
  88.0 1.5 %copy.11 = bf16[32,1536]{1,0:T(8,128)(2,1)} copy(bf16[32,1536]{1,0:T(8,128)(2,1)} %get-tuple-element.6) | data formatting | bytes 196608
  89.5 0.0 copy-start
  89.5 3.4 %copy.12 = bf16[1536,768]{1,0:T(8,128)(2,1)} copy(bf16[1536,768]{1,0:T(8,128)(2,1)} %get-tuple-element.7) | data formatting | bytes 4718592
  92.9 0.0 copy-done
  92.9 1.4 %copy.13 = bf16[768,1536]{1,0:T(8,128)(2,1)} copy(bf16[768,1536]{1,0:T(8,128)(2,1)S(1)} %copy-done) | data formatting | bytes 4718592
Async XLA Ops:
  89.5 3.4 %copy-start = (bf16[768,1536]{1,0:T(8,128)(2,1)S(1)}, bf16[768,1536]{1,0:T(8,128)(2,1)}, u32[]{:S(2)}) copy-start(bf16[768,1536]{1,0:T(8,128)(2,1)} %get-tuple-element.8) | copy-start | bytes 7077892

commit v3 on v2

--- a/solution.py
+++ b/solution.py
@@ -13,6 +13,8 @@
 TN = (((0,), (0,)), ((), ()))
 NN = (((1,), (0,)), ((), ()))
 NTILE = 256
+PTILE = 768
+VMEM_MIB = 46
 SIGN = (1, -1)
 
 RATE = 45500.0
@@ -20,7 +22,35 @@
 HOP, HOP2 = 2.4, 0.65
 CORE_HOP = 1.0
 PRIO1 = 0.6
-GATE_Y, GATE_B, GATE_BY = ("arr", 0, 0, 0, 4, 2), ("By", 0, 3), ("By", 0, 4)
+GATE_Y, GATE_B = ("Byr", 0, 3, 0), ("arr", 0, 0, 2, 4)
+GATE_BY = (("Byr", 0, 4, 0), ("d", 2), ("d", 2), ("ys", 3), ("Byr", 0, 4, 0))
+GATHER = ("y", "zB", "zA", "arr", "By", "Byr", "blk")
+PRIO = {
+    ("arr", 1): 0.4,
+    ("By", 1): 5.2,
+    ("Byr", 1): 3,
+    ("zA", 1): 1.5,
+    ("zB", 1): 3,
+    ("y", 1): 1.5,
+    ("rzt", False): 0.2,
+    ("zB", 0): 0.4,
+    "ys": 3,
+    "s": 0.7,
+    "h": 0.4,
+    "v": 5.2,
+    ("zA", 0): 0.2,
+    "sumA": 0.7,
+    ("arr", 0): 0.7,
+    ("y", 0): 3,
+    ("rzt", True): 0.4,
+    "f": 0,
+    ("Byr", 0): 1.5,
+    ("By", 0): 0.7,
+    "d": 0,
+    "p": 0.7,
+    "e": 1.5,
+    "yc": 1.5,
+}
 
 
 class Task:
@@ -78,7 +108,7 @@
 
 
 def plan(dims, pos, r):
-    NZ, NY, NX, T, W, F, bounds, NA = dims
+    NZ, NY, NX, T, W, F, split, bounds, NA = dims
     NQ = len(bounds) - 1
     z, y, x, c = pos
     HOPS, BT, XT, FH, WH = NZ // 2, NY * T, NY * T // NX, F // 2, W // 2
@@ -119,9 +149,8 @@
 
     A, B = pl.ds(0, bounds[NA]), pl.ds(bounds[NA], W - bounds[NA])
     AW, BW = bounds[NA], W - bounds[NA]
-    mid = bounds[NA // 2]
-    GA = (pl.ds(0, mid), pl.ds(mid, AW - mid))
-    GB = (qs(NA), qs(NA + 1))
+    mid, cut, mid_b = split
+    GAA, GBB = pl.ds(0, cut), pl.ds(cut, W - cut)
     QA, QB = tuple(range(NA)), (NA, NA + 1)
     YD = ((1, 0), (3, 1), (2, None))
 
@@ -136,78 +165,83 @@
 
     def gather(p, own, buf, gate_y, gate_b, gate_by):
         ld = ("load", p)
+        gq, GN = (0, mid, cut, mid_b, W), 2
+        width = lambda q: gq[q + 1] - gq[q]
+        gs = lambda q: pl.ds(gq[q], width(q))
         for j, d in YD:
-            msg(("yo", p, j), YL if d is None else (YL[d],), T * AW * 2,
-                lambda j=j: (r[own].at[:, A], r[buf].at[z, y, :, A], ydev(j)), lambda j=j: r[buf].at[z, yof(-j), :, A])
+            msg(("yo", p, j), YL if d is None else (YL[d],), T * cut * 2,
+                lambda j=j: (r[own].at[:, GAA], r[buf].at[z, y, :, GAA], ydev(j)), lambda j=j: r[buf].at[z, yof(-j), :, GAA])
         yo = [("yo", p, j) for j in (1, 3, 2)]
-        task(("y", p), deps=gate_y, sends=yo, prio=0)
-        for i in range(4):
-            for q in (0, 1):
-                cols = pl.ds(q * WH, WH) if i == 0 else GA[q]
-                pick = lambda b, i=i, cols=cols: r[buf].at[b, yof(-i), :, cols]
-                for d, h in chains(q):
-                    s = SIGN[d]
-                    zb = lambda k, s=s: zof(-s * k)
-                    if i == 0 and h == 1:
-                        make = lambda s=s, pick=pick, cols=cols: (r[own].at[:, cols], pick(z), zdev(s))
-                    else:
-                        make = lambda h=h, s=s, pick=pick, zb=zb: (pick(zb(h - 1)), pick(zb(h - 1)), zdev(s))
-                    msg(("gz", p, d, q, h, i), (ZL[d],), T * cols.size * 2, make, lambda h=h, pick=pick, zb=zb: pick(zb(h)))
-                    nxt = [("gz", p, d, q, h + 1, i)] if h < limit(d, q) else []
-                    dep = ("arr", p, d, q, h - 1, i) if h > 1 else ("zA", p, i) if i else ("zB", p)
-                    task(("arr", p, d, q, h, i), waits=[("gz", p, d, q, h, i)], sends=nxt, prio=0 + p * PRIO1, deps=[dep])
-        first = lambda i: [("gz", p, d, q, 1, i) for q in (0, 1) for d in (0, 1) if limit(d, q) >= 1]
-        task(("zB", p), deps=gate_b, sends=first(0), prio=0)
-        for i in (1, 3, 2):
-            task(("zA", p, i), deps=[("y", p)], waits=[("yo", p, i)], sends=first(i), prio=0)
+        task(("y", p), deps=gate_y, sends=yo, prio=p * PRIO1)
+        for q in range(4):
+            for d, h in chains(q):
+                s = SIGN[d]
+                zb = lambda k, s=s: zof(-s * k)
+                if q < GN:
+                    pick = lambda b, q=q: r[buf].at[b, :, :, gs(q)]
+                else:
+                    pick = lambda b, q=q: r[buf].at[b, y, :, gs(q)]
+                if h == 1 and q >= GN:
+                    make = lambda q=q, s=s, pick=pick: (r[own].at[:, gs(q)], pick(z), zdev(s))
+                else:
+                    make = lambda h=h, s=s, pick=pick, zb=zb: (pick(zb(h - 1)), pick(zb(h - 1)), zdev(s))
+                msg(("gz", p, d, q, h), (ZL[d],), (BT if q < GN else T) * width(q) * 2, make,
+                    lambda h=h, pick=pick, zb=zb: pick(zb(h)))
+                nxt = [("gz", p, d, q, h + 1)] if h < limit(d, q) else []
+                task(("arr", p, d, q, h), waits=[("gz", p, d, q, h)], sends=nxt, prio=0,
+                     deps=[("arr", p, d, q, h - 1)] if h > 1 else [("zA", p) if q < GN else ("zB", p)])
+        first = lambda qq: [("gz", p, d, q, 1) for q in qq for d in (0, 1) if limit(d, q) >= 1]
+        task(("zB", p), deps=gate_b, sends=first((2, 3)), prio=p * PRIO1)
+        task(("zA", p), deps=[("y", p)], waits=yo + [ld], sends=first((0, 1)), prio=p * PRIO1)
         for k in range(NZ):
-            come = [[], []]
-            for i in range(4 if k else 0):
-                for q in (0, 1):
-                    at = ("arr", p, 1, q, k, i) if k <= limit(1, q) else ("arr", p, 0, q, NZ - k, i)
-                    come[i > 0].append(at)
+            come = []
+            for q in range(4 if k else 0):
+                come.append(("arr", p, 1, q, k) if k <= limit(1, q) else ("arr", p, 0, q, NZ - k))
             for d in (0, 1):
                 s = SIGN[d]
-                msg(("by", p, k, d), (YL[d],), T * BW * 2,
-                    lambda s=s, k=k: (r[buf].at[zof(k), y, :, B] if k else r[own].at[:, B], r[buf].at[zof(k), y, :, B], ydev(s)),
-                    lambda s=s, k=k: r[buf].at[zof(k), yof(-s), :, B])
+                msg(("by", p, k, d), (YL[d],), T * (W - cut) * 2,
+                    lambda s=s, k=k: (r[buf].at[zof(k), y, :, GBB] if k else r[own].at[:, GBB], r[buf].at[zof(k), y, :, GBB], ydev(s)),
+                    lambda s=s, k=k: r[buf].at[zof(k), yof(-s), :, GBB])
                 fwd = lambda s, k, cols: r[buf].at[zof(k), yof(-s), :, cols]
-                cols = GB[d]
-                msg(("byr", p, k, d), (YL[d],), T * cols.size * 2,
+                cols = gs(GN + d)
+                msg(("byr", p, k, d), (YL[d],), T * width(GN + d) * 2,
                     lambda s=s, k=k, cols=cols, fwd=fwd: (fwd(s, k, cols), fwd(s, k, cols), ydev(s)),
                     lambda k=k, cols=cols: r[buf].at[zof(k), yof(-2), :, cols])
-            task(("By", p, k), deps=(come[0] if k else [("y", p)]) + gate_by,
+            task(("By", p, k), deps=(come[GN:] if k else [("y", p)]) + gate_by[min(k, NZ - k)],
                  sends=[("by", p, k, 0), ("by", p, k, 1)], prio=p * PRIO1)
             for d in (0, 1):
-                task(("Byr", p, k, d), deps=[("By", p, k)], waits=[("by", p, k, d)], sends=[("byr", p, k, d)],
-                     prio=p * PRIO1)
-            task(("blk", p, k), deps=(come[1] if k else [("zA", p, i) for i in (1, 2, 3)]) + [("Byr", p, k, 0), ("Byr", p, k, 1)],
-                 waits=[("byr", p, k, 0), ("byr", p, k, 1)] + ([] if k else [ld]), prio=p * PRIO1)
-
-    gather(0, "grad", "G", [], [], [])
-    known = {t.name for t in tasks}
-    gates = [[g] if g in known else [("zB", 0)] for g in (GATE_Y, GATE_B, GATE_BY)]
-    gather(1, "inp", "I", *gates)
+                task(("Byr", p, k, d), deps=[("By", p, k)], waits=[("by", p, k, d)], sends=[("byr", p, k, d)], prio=p * PRIO1)
+            task(("blk", p, k), deps=(come[:GN] if k else [("zA", p)]) + [("Byr", p, k, 0), ("Byr", p, k, 1)],
+                 waits=[("byr", p, k, 0), ("byr", p, k, 1)], prio=p * PRIO1)
+
+    gather(0, "grad", "G", [], [], [[]] * (HOPS + 1))
+    gather(1, "inp", "I", [GATE_Y], [GATE_B], [[g] for g in GATE_BY])
     for i in range(2, 5):
         task(("ld", i), waits=[("load", i)], cost=0, prio=1)
 
+    def both(k):
+        return (k,) if k in (0, HOPS) else (k, NZ - k)
+
     def dot_d(k):
-        zb = zof(k)
-        lhs = r["G"][zb].reshape(BT, W)
-
-        @pl.loop(0, F // NTILE)
-        def _(n):
-            cols = pl.ds(pl.multiple_of(n * NTILE, NTILE), NTILE)
-            v = lax.dot_general(lhs, r["WO"][cols, :], NT, preferred_element_type=F32)
-            r["D"][zb, :, :, cols] = v.reshape(NX, XT, NTILE)
+        zbs = [zof(i) for i in both(k)]
+        lhs = jnp.concatenate([r["G"][zb].reshape(BT, W) for zb in zbs], axis=0)
+        v = lax.dot_general(lhs, r["WO"][...], NT, preferred_element_type=F32)
+        for i, zb in enumerate(zbs):
+            r["D"][zb] = v[i * BT:(i + 1) * BT].reshape(NX, XT, F)
+
+    def narrow(k):
+        return min(k, NZ - k) >= 2
 
     def sum_core(k):
-        r["XS"][k] = r["D"][zof(k), :, :, half(c)] + r["PR"][k]
+        v = r["D"][zof(k), :, :, half(c)] + r["PR"][k]
+        r["XS"][k] = v
+        if narrow(k):
+            r["XB"][k] = v.astype(BF16)
 
     def make_dh(k):
         v = r["XS"][k, x]
         for j in range(1, NX):
-            v = v + r["XR"][k, j - 1]
+            v = v + (r["XC"][k, j - 1].astype(F32) if narrow(k) else r["XR"][k, j - 1])
         zb = zof(k)
         h = r["H"][pl.ds(pl.multiple_of(zb * BT + x * XT, XT), XT), half(c)].astype(F32)
         t = gelu_tanh(h)
@@ -218,8 +252,10 @@
         msg(("pair", k), ("core",), BT * FH * 4,
             lambda k=k: (r["D"].at[zof(k), :, :, half(1 - c)], r["PR"].at[k], core), lambda k=k: r["PR"].at[k])
         for j in range(1, NX):
-            msg(("xs", k, j), xlinks(j), XT * FH * 4,
-                lambda k=k, j=j: (r["XS"].at[k, xof(j)], r["XR"].at[k, j - 1], xdev(j)), lambda k=k, j=j: r["XR"].at[k, j - 1])
+            a, b = ("XB", "XC") if narrow(k) else ("XS", "XR")
+            msg(("xs", k, j), xlinks(j), XT * FH * (2 if narrow(k) else 4),
+                lambda k=k, j=j, a=a, b=b: (r[a].at[k, xof(j)], r[b].at[k, j - 1], xdev(j)),
+                lambda k=k, j=j, b=b: r[b].at[k, j - 1])
             msg(("dh", k, j), xlinks(j), XT * FH * 2,
                 lambda k=k, j=j: (r["DH"].at[zof(k), x, :, half(c)], r["DH"].at[zof(k), x, :, half(c)], xdev(j)),
                 lambda k=k, j=j: r["DH"].at[zof(k), xof(-j), :, half(c)])
@@ -227,23 +263,24 @@
             lambda k=k: (r["DH"].at[zof(k), :, :, half(c)], r["DH"].at[zof(k), :, :, half(c)], core),
             lambda k=k: r["DH"].at[zof(k), :, :, half(1 - c)])
         peers = range(1, NX)
-        task(("d", k), deps=[("blk", 0, k), ("ld", 3)], sends=[("pair", k)], cost=1.2, prio=1, run=lambda k=k: dot_d(k))
-        task(("s", k), deps=[("d", k)], waits=[("pair", k)], sends=[("xs", k, j) for j in peers], cost=0.3, prio=0.5,
+        first = min(k, NZ - k) if k else 0
+        if k == first:
+            task(("d", k), deps=[("blk", 0, i) for i in both(k)] + [("ld", 3)], sends=[("pair", i) for i in both(k)],
+                 cost=0.9, prio=1, run=lambda k=k: dot_d(k))
+        task(("s", k), deps=[("d", first)], waits=[("pair", k)], sends=[("xs", k, j) for j in peers], cost=0.15, prio=0.5,
              run=lambda k=k: sum_core(k))
         task(("h", k), deps=[("s", k), ("ld", 2)], waits=[("xs", k, j) for j in peers],
-             sends=[("dh", k, j) for j in peers], cost=0.3, prio=0.5, run=lambda k=k: make_dh(k))
+             sends=[("dh", k, j) for j in peers], cost=0.2, prio=0.5, run=lambda k=k: make_dh(k))
         task(("f", k), deps=[("h", k)], waits=[("dh", k, j) for j in peers], sends=[("df", k)], prio=0.5)
         task(("e", k), deps=[("f", k)], waits=[("df", k)], prio=0.5)
 
     def dot_p(k):
-        zb = zof(k)
-        lhs = r["DH"][zb].reshape(BT, F)
-
-        @pl.loop(0, W // NTILE)
-        def _(n):
-            cols = pl.ds(pl.multiple_of(n * NTILE, NTILE), NTILE)
-            v = lax.dot_general(lhs, r["WI"][cols, :], NT, preferred_element_type=F32)
-            r["PF"][zb, :, :, cols] = v.reshape(NY, T, NTILE)
+        zbs = [zof(i) for i in both(k)]
+        lhs = jnp.concatenate([r["DH"][zb].reshape(BT, F) for zb in zbs], axis=0)
+        for n in range(0, W, PTILE):
+            v = lax.dot_general(lhs, r["WI"][n:n + PTILE, :], NT, preferred_element_type=F32)
+            for i, zb in enumerate(zbs):
+                r["PF"][zb, :, :, n:n + PTILE] = v[i * BT:(i + 1) * BT].reshape(NY, T, PTILE)
 
     def ystage(key, k, qq, dep, cost):
         slot = k
@@ -312,8 +349,11 @@
         r["BS"][tag(q, d, h), :, pl.ds(0, qw(q))] = v.astype(BF16)
 
     for n, k in enumerate(order):
-        task(("p", k), deps=[("e", k), ("ld", 4)], cost=1.2, prio=1 + 0.01 * n, run=lambda k=k: dot_p(k))
-        waits, total = ystage(k, k, QB, [("p", k)], 0.2)
+        first = min(k, NZ - k) if k else 0
+        if k == first:
+            task(("p", k), deps=[("e", i) for i in both(k)] + [("ld", 4)], cost=1.1, prio=1 + 0.01 * n,
+                 run=lambda k=k: dot_p(k))
+        waits, total = ystage(k, k, QB, [("p", first)], 0.15)
 
         def hold(k=k, total=total):
             r["VB"][k] = total()
@@ -326,7 +366,7 @@
                 waits = [("rz", d, q, h + 1)] if h < limit(d, q) else []
                 dep = [("rzt", d, q, h + 1)] if h < limit(d, q) else []
                 if q < NA:
-                    task(("rzt", d, q, h), deps=dep + [("p", k)], waits=waits, sends=[("rz", d, q, h)], cost=0.12,
+                    task(("rzt", d, q, h), deps=dep + [("p", first)], waits=waits, sends=[("rz", d, q, h)], cost=0.08,
                          prio=0.3, run=lambda d=d, q=q, h=h: step_a(d, q, h))
                 else:
                     task(("rzt", d, q, h), deps=dep + [("v", k)], waits=waits, sends=[("rz", d, q, h)], cost=0.05,
@@ -365,7 +405,7 @@
             r["OUT"][:, qs(q)] = v.astype(BF16)
 
     task("outB", deps=[("v", 0)] + sent(QB), waits=lasts(QB), cost=0.1, prio=0.3, run=out_b)
-    task("out", deps=["outA", "outB"], cost=0.05, run=lambda: r["store"](2))
+    task("out", deps=["outA", "outB"], cost=0.05)
 
     def act_piece(i):
         rows = pl.ds(i * BT, BT)
@@ -384,15 +424,25 @@
         r["GI"][cols, :] = lax.dot_general(lhs, rhs, TN, preferred_element_type=F32).astype(BF16)
 
     for i in range(NZ):
-        task(("act", i), deps=[("ld", 2)], cost=0.6, prio=5, run=lambda i=i: act_piece(i))
+        task(("act", i), deps=[("ld", 2)], cost=0.25, prio=5, run=lambda i=i: act_piece(i))
     for n in range(W // NTILE):
-        task(("go", n), deps=[("blk", 0, k) for k in range(NZ)] + [("act", i) for i in range(NZ)], cost=0.9, prio=6,
+        task(("go", n), deps=[("blk", 0, k) for k in range(NZ)] + [("act", i) for i in range(NZ)], cost=0.6, prio=6,
              run=lambda n=n: gwo_piece(n))
-    task("goout", deps=[("go", n) for n in range(W // NTILE)], prio=6, run=lambda: r["store"](0))
+    task("goout", deps=[("go", n) for n in range(W // NTILE)], prio=6)
     for n in range(W // NTILE):
-        task(("gi", n), deps=[("blk", 1, k) for k in range(NZ)] + [("e", k) for k in range(NZ)], cost=1.0, prio=7,
+        task(("gi", n), deps=[("blk", 1, k) for k in range(NZ)] + [("e", k) for k in range(NZ)], cost=0.65, prio=7,
              run=lambda n=n: gwi_piece(n))
-    task("giout", deps=[("gi", n) for n in range(W // NTILE)], prio=7, run=lambda: r["store"](1))
+    task("giout", deps=[("gi", n) for n in range(W // NTILE)], prio=7)
+    known = {t.name for t in tasks}
+    for t in tasks:
+        t.deps = tuple(d for d in t.deps if d in known)
+        n = t.name
+        kind = n if isinstance(n, str) else n[0]
+        if kind in GATHER:
+            kind = (kind, n[1])
+        elif kind == "rzt":
+            kind = (kind, n[2] < NA)
+        t.prio = PRIO.get(kind, t.prio)
     return tasks, msgs
 
 
@@ -402,8 +452,8 @@
 
 
 LOADS = {("load", 0): 0.5, ("load", 1): 0.5, ("load", 2): 1.5, ("load", 3): 3.0, ("load", 4): 4.5}
-NAMES = ("inp", "hid", "grad", "w_in", "w_out", "g_in", "gw_in", "gw_out", "G", "I", "H", "WI", "WO", "AT", "D", "PR", "XS",
-         "XR", "DH", "PF", "AS", "AR", "YS", "YR", "YA", "AY", "VB", "BS", "BR", "OUT", "GI", "GO", "loc", "osem", "ss", "rs")
+NAMES = ("inp", "hid", "grad", "w_in", "w_out", "OUT", "GI", "GO", "G", "I", "H", "WI", "WO", "AT", "D", "PR", "XS",
+         "XR", "XB", "XC", "DH", "PF", "AS", "AR", "YS", "YR", "YA", "AY", "VB", "BS", "BR", "loc", "ss", "rs")
 
 
 def kernel(dims, *refs):
@@ -417,10 +467,6 @@
     copies = [pltpu.make_async_copy(a, b, r["loc"].at[i]) for i, (a, b) in enumerate(copies)]
     for cp in copies:
         cp.start()
-    stores = [pltpu.make_async_copy(a, b, r["osem"].at[i]) for i, (a, b) in enumerate(
-        [(r["GO"], r["gw_out"]), (r["GI"], r["gw_in"]), (r["OUT"], r["g_in"])])]
-    r["store"] = lambda i: stores[i].start()
-
     tasks, msgs = plan(dims, (z, y, x, c), r)
     order = order_of(tasks, msgs, LOADS)[0]
 
@@ -454,12 +500,18 @@
             started.append(cp)
     for cp in started:
         cp.wait_send()
-    for cp in stores:
+
+
+def store(*refs):
+    copies = [pltpu.make_async_copy(refs[i], refs[3 + i], refs[6].at[i]) for i in range(3)]
+    for cp in copies:
+        cp.start()
+    for cp in copies:
         cp.wait()
 
 
 def build(dims):
-    NZ, NY, NX, T, W, F, bounds, NA = dims
+    NZ, NY, NX, T, W, F, split, bounds, NA = dims
     HOPS, BT = NZ // 2, NY * T
     XT, FH = BT // NX, F // 2
     AW, BW = bounds[NA], W - bounds[NA]
@@ -469,15 +521,12 @@
     def body(inputs, hidden_pre, out_grad, weight_in, weight_out):
         any_spec = pl.BlockSpec(memory_space=pl.ANY)
         vm, dma, n = pltpu.VMEM, pltpu.SemaphoreType.DMA, n_msgs(dims)
-        return pl.pallas_call(
+        shapes = tuple(jax.ShapeDtypeStruct(v, BF16) for v in ((T, W), (W, F), (F, W)))
+        outs = pl.pallas_call(
             functools.partial(kernel, dims),
-            out_shape=(
-                jax.ShapeDtypeStruct((T, W), BF16),
-                jax.ShapeDtypeStruct((W, F), BF16),
-                jax.ShapeDtypeStruct((F, W), BF16),
-            ),
+            out_shape=shapes,
             in_specs=[any_spec] * 5,
-            out_specs=(any_spec,) * 3,
+            out_specs=(pl.BlockSpec(memory_space=pltpu.VMEM),) * 3,
             scratch_shapes=[
                 vm((NZ, NY, T, W), BF16),
                 vm((NZ, NY, T, W), BF16),
@@ -489,6 +538,8 @@
                 vm((NZ, NX, XT, FH), F32),
                 vm((NZ, NX, XT, FH), F32),
                 vm((NZ, NX - 1, XT, FH), F32),
+                vm((NZ, NX, XT, FH), BF16),
+                vm((NZ, NX - 1, XT, FH), BF16),
                 vm((NZ, NX, XT, F), BF16),
                 vm((NZ, NY, T, W), F32),
                 vm((2 * NA * HOPS, NY, T, QA), BF16),
@@ -500,25 +551,29 @@
                 vm((NZ, T, BW), F32),
                 vm((2 * NA * HOPS, T, QB), BF16),
                 vm((2 * NA * HOPS, T, QB), BF16),
-                vm((T, W), BF16),
-                vm((W, F), BF16),
-                vm((F, W), BF16),
                 dma((5,)),
-                dma((3,)),
                 dma((n,)),
                 dma((n,)),
             ],
             compiler_params=pltpu.CompilerParams(
-                collective_id=0, has_side_effects=True, vmem_limit_bytes=60 * 2**20
+                collective_id=0, has_side_effects=True, vmem_limit_bytes=VMEM_MIB * 2**20
             ),
         )(inputs, hidden_pre, out_grad, weight_in, weight_out)
+        return pl.pallas_call(
+            store,
+            out_shape=shapes,
+            in_specs=[pl.BlockSpec(memory_space=pltpu.VMEM)] * 3,
+            out_specs=(any_spec,) * 3,
+            scratch_shapes=[dma((3,))],
+            compiler_params=pltpu.CompilerParams(vmem_limit_bytes=8 * 2**20),
+        )(*outs)
 
     return body
 
 
 def solution(mesh):
     return jax.shard_map(
-        build((8, 4, 4, 32, 1536, 768, (0, 256, 384, 512, 640, 1024, 1536), 4)),
+        build((8, 4, 4, 32, 1536, 768, (256, 512, 1024), (0, 256, 512, 640, 768, 1152, 1536), 4)),
         mesh=mesh,
         in_specs=(
             P("row", "col"),

time: 95 us -> 85.4 us (0.90)
  Pallas kernels: 87.4 us -> 81.2 us
  local copies, waits for them, and re-layouts: 6.32 us -> 3.19 us
    pallas_call x1 -> x2, Pallas kernels: 87.4 us -> 81.2 us  [the longest x1 79 us: body(): pl.pallas_call(functools.partial(kernel, dims), out_shape=shapes, in_spec...]
    unnamed x5 -> x6, local copies, waits for them, and re-layouts: 6.32 us -> 3.19 us
where the time goes in v3:
time: 85.4 us; the launch traced here: 85.2 us
  Pallas kernels  81.2 us (95%)
  local copies, waits for them, and re-layouts  3.19 us (4%)
    pallas_call x1, Pallas kernels, body(): pl.pallas_call(functools.partial(kernel, dims), out_shape=shapes, in_spec...  79 us
    unnamed x6, local copies, waits for them, and re-layouts  3.19 us
    pallas_call x1, Pallas kernels, body(): pl.pallas_call(store, out_shape=shapes, in_specs=[pl.BlockSpec(memory_spa...  2.24 us

profile of v3, /device:TPU:32, one launch (start us, length us, event | category | flops | bytes accessed | tf_op | source)
XLA Modules:
  0.0 85.2 jit_solution(16474354111474402283)
XLA Ops:
  0.6 0.0 copy-start
  0.6 1.4 %copy-done = bf16[1024,768]{1,0:T(8,128)(2,1)S(1)} copy-done((bf16[1024,768]{1,0:T(8,128)(2,1)S(1)}, bf16[1024,768]{1,0:T(8,128)(2,1)}, u32[]{:S(2)}) %copy-start) | copy-done | bytes 1572888
  2.0 0.0 copy-start.1
  2.0 0.9 %copy-done.1 = bf16[32,1536]{1,0:T(8,128)(2,1)S(1)} copy-done((bf16[32,1536]{1,0:T(8,128)(2,1)S(1)}, bf16[32,1536]{1,0:T(8,128)(2,1)}, u32[]{:S(2)}) %copy-start.1) | copy-done | bytes 98328
  2.9 0.0 copy-start.2
  2.9 0.9 %copy-done.2 = bf16[32,1536]{1,0:T(8,128)(2,1)S(1)} copy-done((bf16[32,1536]{1,0:T(8,128)(2,1)S(1)}, bf16[32,1536]{1,0:T(8,128)(2,1)}, u32[]{:S(2)}) %copy-start.2) | copy-done | bytes 98328
  3.8 79.0 %shard_map.76 = (bf16[32,1536]{1,0:T(8,128)(2,1)S(1)}, bf16[1536,768]{1,0:T(8,128)(2,1)S(1)}, bf16[768,1536]{1,0:T(8,128)(2,1)S(1)}) custom-call(bf16[32,1536]{1,0:T(8,128)(2,1)S(1)} %copy-done.1, bf16[1024,768]{1,0:T(8,128)(2,1)S(1)} %copy-done, bf16[32,1536]{1,0:T(8,128)(2,1)S(1)} %copy-done.2, bf16[1536,768]{1,0:T(8,128)(2,1)} %refs_3_.1, ...), custom_call_target="tpu_custom_call" | custom-call | tf_op jit(solution)/shard_map/pallas_call | solution.py:525
  82.8 2.2 %shard_map.77 = (bf16[32,1536]{1,0:T(8,128)(2,1)}, bf16[1536,768]{1,0:T(8,128)(2,1)}, bf16[768,1536]{1,0:T(8,128)(2,1)}) custom-call(bf16[32,1536]{1,0:T(8,128)(2,1)S(1)} %get-tuple-element.6.refs_0_, bf16[1536,768]{1,0:T(8,128)(2,1)S(1)} %get-tuple-element.7.refs_1_, bf16[768,1536]{1,0:T(8,128)(2,1)S(1)} %get-tuple-element.8.refs_2_), custom_call_target="tpu_custom_call" | custom-call | tf_op jit(solution)/shard_map/pallas_call | solution.py:562
Async XLA Ops:
  0.6 1.4 %copy-start = (bf16[1024,768]{1,0:T(8,128)(2,1)S(1)}, bf16[1024,768]{1,0:T(8,128)(2,1)}, u32[]{:S(2)}) copy-start(bf16[1024,768]{1,0:T(8,128)(2,1)} %refs_1_.1) | copy-start | bytes 4718596
  2.0 0.9 %copy-start.1 = (bf16[32,1536]{1,0:T(8,128)(2,1)S(1)}, bf16[32,1536]{1,0:T(8,128)(2,1)}, u32[]{:S(2)}) copy-start(bf16[32,1536]{1,0:T(8,128)(2,1)} %refs_0_.1) | copy-start | bytes 294916
  2.9 0.9 %copy-start.2 = (bf16[32,1536]{1,0:T(8,128)(2,1)S(1)}, bf16[32,1536]{1,0:T(8,128)(2,1)}, u32[]{:S(2)}) copy-start(bf16[32,1536]{1,0:T(8,128)(2,1)} %refs_2_.1) | copy-start | bytes 294916

commit v4 on v3

--- a/solution.py
+++ b/solution.py
@@ -558,7 +558,8 @@
             compiler_params=pltpu.CompilerParams(
                 collective_id=0, has_side_effects=True, vmem_limit_bytes=VMEM_MIB * 2**20
             ),
-        )(inputs, hidden_pre, out_grad, weight_in, weight_out)
+        )(*(pltpu.with_memory_space_constraint(v, pltpu.MemorySpace.HBM)
+            for v in (inputs, hidden_pre, out_grad, weight_in, weight_out)))
         return pl.pallas_call(
             store,
             out_shape=shapes,

time: 85.4 us -> 82.2 us (0.963)
  local copies, waits for them, and re-layouts: 3.19 us -> 0 us
    unnamed x6 -> x0, local copies, waits for them, and re-layouts: 3.19 us -> none
where the time goes in v4:
time: 82.2 us; the launch traced here: 82.1 us
  Pallas kernels  81.3 us (99%)
    pallas_call x1, Pallas kernels, body(): pl.pallas_call(functools.partial(kernel, dims), out_shape=shapes, in_spec...  79.1 us
    pallas_call x1, Pallas kernels, body(): pl.pallas_call(store, out_shape=shapes, in_specs=[pl.BlockSpec(memory_spa...  2.24 us

profile of v4, /device:TPU:32, one launch (start us, length us, event | category | flops | bytes accessed | tf_op | source)
XLA Modules:
  0.0 82.1 jit_solution(7497157218558868695)
XLA Ops:
  0.6 79.1 %shard_map.76 = (bf16[32,1536]{1,0:T(8,128)(2,1)S(1)}, bf16[1536,768]{1,0:T(8,128)(2,1)S(1)}, bf16[768,1536]{1,0:T(8,128)(2,1)S(1)}) custom-call(bf16[32,1536]{1,0:T(8,128)(2,1)} %refs_0_.1, bf16[1024,768]{1,0:T(8,128)(2,1)} %refs_1_.1, bf16[32,1536]{1,0:T(8,128)(2,1)} %refs_2_.1, bf16[1536,768]{1,0:T(8,128)(2,1)} %refs_3_.1, bf16[768,1536]{1,0:T(8,128)(2,1)} %refs_4_.1), custom_call_target="tpu_custom_call" | custom-call | tf_op jit(solution)/shard_map/pallas_call | solution.py:525
  79.7 2.2 %shard_map.77 = (bf16[32,1536]{1,0:T(8,128)(2,1)}, bf16[1536,768]{1,0:T(8,128)(2,1)}, bf16[768,1536]{1,0:T(8,128)(2,1)}) custom-call(bf16[32,1536]{1,0:T(8,128)(2,1)S(1)} %get-tuple-element.6.refs_0_, bf16[1536,768]{1,0:T(8,128)(2,1)S(1)} %get-tuple-element.7.refs_1_, bf16[768,1536]{1,0:T(8,128)(2,1)S(1)} %get-tuple-element.8.refs_2_), custom_call_target="tpu_custom_call" | custom-call | tf_op jit(solution)/shard_map/pallas_call | solution.py:563

commit v5 on v4

--- a/solution.py
+++ b/solution.py
@@ -14,6 +14,7 @@
 NN = (((1,), (0,)), ((), ()))
 NTILE = 256
 PTILE = 768
+PARTS = (1, 6, 6)
 VMEM_MIB = 46
 SIGN = (1, -1)
 
@@ -503,7 +504,12 @@
 
 
 def store(*refs):
-    copies = [pltpu.make_async_copy(refs[i], refs[3 + i], refs[6].at[i]) for i in range(3)]
+    copies = []
+    for i in range(3):
+        step = refs[i].shape[0] // PARTS[i]
+        for n in range(PARTS[i]):
+            rows = pl.ds(n * step, step)
+            copies.append(pltpu.make_async_copy(refs[i].at[rows], refs[3 + i].at[rows], refs[6].at[len(copies)]))
     for cp in copies:
         cp.start()
     for cp in copies:
@@ -565,7 +571,7 @@
             out_shape=shapes,
             in_specs=[pl.BlockSpec(memory_space=pltpu.VMEM)] * 3,
             out_specs=(any_spec,) * 3,
-            scratch_shapes=[dma((3,))],
+            scratch_shapes=[dma((sum(PARTS),))],
             compiler_params=pltpu.CompilerParams(vmem_limit_bytes=8 * 2**20),
         )(*outs)
 

time: 82.2 us -> 82.3 us (level)
  no operation moved by 1% of the time
where the time goes in v5:
time: 82.3 us; the launch traced here: 82.2 us
  Pallas kernels  81.4 us (99%)
    pallas_call x1, Pallas kernels, body(): pl.pallas_call(functools.partial(kernel, dims), out_shape=shapes, in_spec...  79.1 us
    pallas_call x1, Pallas kernels, body(): pl.pallas_call(store, out_shape=shapes, in_specs=[pl.BlockSpec(memory_spa...  2.32 us

profile of v5, /device:TPU:32, one launch (start us, length us, event | category | flops | bytes accessed | tf_op | source)
XLA Modules:
  0.0 82.2 jit_solution(2243847574324032705)
XLA Ops:
  0.6 79.1 %shard_map.76 = (bf16[32,1536]{1,0:T(8,128)(2,1)S(1)}, bf16[1536,768]{1,0:T(8,128)(2,1)S(1)}, bf16[768,1536]{1,0:T(8,128)(2,1)S(1)}) custom-call(bf16[32,1536]{1,0:T(8,128)(2,1)} %refs_0_.1, bf16[1024,768]{1,0:T(8,128)(2,1)} %refs_1_.1, bf16[32,1536]{1,0:T(8,128)(2,1)} %refs_2_.1, bf16[1536,768]{1,0:T(8,128)(2,1)} %refs_3_.1, bf16[768,1536]{1,0:T(8,128)(2,1)} %refs_4_.1), custom_call_target="tpu_custom_call" | custom-call | tf_op jit(solution)/shard_map/pallas_call | solution.py:531
  79.7 2.3 %shard_map.77 = (bf16[32,1536]{1,0:T(8,128)(2,1)}, bf16[1536,768]{1,0:T(8,128)(2,1)}, bf16[768,1536]{1,0:T(8,128)(2,1)}) custom-call(bf16[32,1536]{1,0:T(8,128)(2,1)S(1)} %get-tuple-element.6.refs_0_, bf16[1536,768]{1,0:T(8,128)(2,1)S(1)} %get-tuple-element.7.refs_1_, bf16[768,1536]{1,0:T(8,128)(2,1)S(1)} %get-tuple-element.8.refs_2_), custom_call_target="tpu_custom_call" | custom-call | tf_op jit(solution)/shard_map/pallas_call | solution.py:569
